TPU v7x, 256 devices: a whole 4x4x8 slice. The times are simulated.
256 devices in a mesh: gx: 4 (over y), gy: 16 (over z, core), gz: 4 (over x).
Axes of the slice: x: 4, y: 4, z: 8, core: 2. Of those that a mesh axis runs over, the one named last changes fastest.
Arguments:
- positions: float32 [3, 16, 64, 8, 128], P(None, 'gx', 'gy', 'gz'), may hold values from 0 to 256, as said below
- grain_radii: float32 [16, 64, 8, 128], P('gx', 'gy', 'gz'), may hold values from 0.4 to 0.6
- film_liquid: float32 [16, 64, 8, 128], P('gx', 'gy', 'gz'), may hold values from 0.5 to 2
- pair_live: int32 [4, 16, 4, 864], P('gx', 'gy', 'gz'), may hold values from 0 to 1, as said below
- partner: int32 [4, 16, 4, 864, 128], P('gx', 'gy', 'gz'), may hold values from 0 to 127, as said below
- rupture: int32 [4, 16, 4, 864, 128], P('gx', 'gy', 'gz'), may hold values from 0 to 1
- volume: float32 [4, 16, 4, 864, 128], P('gx', 'gy', 'gz'), may hold values from 0.005 to 0.05
Outputs:
- forces: float32 [3, 16, 64, 8, 128], P(None, 'gx', 'gy', 'gz')
- film_next: float32 [16, 64, 8, 128], P('gx', 'gy', 'gz')
- volume_next: float32 [4, 16, 4, 864, 128], P('gx', 'gy', 'gz')
Inputs may be any that keep to these rules, and one draw needn't show every extreme that they name: `pair_live`: slot s of a device is 1 only if its tile pair lies inside the grid; every pair of distinct touching tiles is listed at most once over all devices, by one of its two tiles; the slot of a tile with itself (s % 27 = 13) is always 1. partner[s, m] is never m itself. `positions`: the grains of tile (p, q, r) lie in its box, 8 wide along the first dimension and 4 along the others, the boxes side by side from the root; no two grains are closer than 0.5.
All inputs are finite; a program needn't handle non-finite values.
Results may differ from a plain program's by a relative error of at most 0.0003.
Values sent between devices are 32-bit elements; how exact they have to be, the bound alone decides.
No kernel may reach another device: no remote copies, remote signals or barrier semaphores. Data moves between devices by JAX's collectives and lax.ppermute only.
A program may use at most 64 MiB of HBM per device.

v0:
```python
import jax
import jax.numpy as jnp
from jax import lax
from jax.sharding import PartitionSpec as P

ABSORB = 0.02
block_tiles = 2


def padded(cells, sides, width):
    for axis, dim in sides:
        count = lax.axis_size(axis)
        ends = count - 1
        head = lax.slice_in_dim(cells, 0, width, axis=dim)
        tail = lax.slice_in_dim(cells, cells.shape[dim] - width, cells.shape[dim], axis=dim)
        cells = jnp.concatenate(
            [
                lax.ppermute(tail, axis, [(i, (i + 1) % count) for i in range(ends)]),
                cells,
                lax.ppermute(head, axis, [((i + 1) % count, i) for i in range(ends)]),
            ],
            axis=dim,
        )
    return cells


def evaluate(pieces):
    anchor, others, centre, active, partner, rupture, volume = pieces
    grains = anchor.shape[-1]
    identity = jnp.eye(grains, dtype=jnp.float32)
    diagonal = identity[None] * centre[:, None, None]
    deltas = [
        anchor[:, component, :, None] - others[:, component, None, :] for component in range(3)
    ]
    squares = deltas[0] * deltas[0] + deltas[1] * deltas[1] + deltas[2] * deltas[2] + diagonal
    distance = jnp.sqrt(squares)
    reach_sum = anchor[:, 3, :, None] + others[:, 3, None, :]
    reduced = anchor[:, 3, :, None] * others[:, 3, None, :] / reach_sum
    intersection = jnp.maximum(reach_sum - distance, 0.0) * (1.0 - diagonal)
    repulse = (
        jnp.sqrt(reduced) * intersection * jnp.sqrt(intersection) / distance * active[:, None, None]
    )
    products = [repulse * member for member in deltas]
    keep_other = (1.0 - centre)[:, None]
    contact_a = jnp.stack([jnp.sum(member, axis=2) for member in products], axis=1)
    contact_b = jnp.stack([-jnp.sum(member, axis=1) * keep_other for member in products], axis=1)
    choose = (partner[:, :, None] == jnp.arange(grains, dtype=jnp.int32)[None, None, :]).astype(
        jnp.float32
    )
    matched = jnp.einsum("ncj,nij->nci", others, choose, precision=lax.Precision.HIGHEST)
    gap_vec = anchor[:, :3] - matched[:, :3]
    spacing = jnp.sqrt(jnp.sum(gap_vec * gap_vec, axis=1))
    radius_sum = anchor[:, 3] + matched[:, 3]
    harmonic = 2.0 * anchor[:, 3] * matched[:, 3] / radius_sum
    scaled_gap = jnp.maximum(spacing - radius_sum, 0.0) * jnp.sqrt(harmonic / volume)
    broken = rupture.astype(jnp.float32)
    intact = active[:, None] * (1.0 - broken)
    tension = (
        intact * harmonic / (1.0 + 1.05 * scaled_gap + 2.5 * scaled_gap * scaled_gap) / spacing
    )
    bridge_force = tension[:, None, :] * gap_vec
    released = active[:, None] * broken * volume
    volume_next = intact * (volume + ABSORB * (anchor[:, 4] + matched[:, 4]))
    liquid_anchor = 0.5 * released - ABSORB * intact * anchor[:, 4]
    liquid_other = 0.5 * released - ABSORB * intact * matched[:, 4]
    reaction = jnp.einsum(
        "nci,nij->ncj",
        jnp.concatenate([bridge_force, liquid_other[:, None]], axis=1),
        choose,
        precision=lax.Precision.HIGHEST,
    )
    anchor_side = jnp.concatenate([contact_a - bridge_force, liquid_anchor[:, None]], axis=1)
    other_side = (
        jnp.concatenate([contact_b, jnp.zeros_like(liquid_anchor)[:, None]], axis=1) + reaction
    )
    return (anchor_side, other_side, volume_next)


def spread_three(terms, axis_dim):
    total = None
    for shift, member in zip((-1, 0, 1), terms):
        widths = [(0, 0)] * member.ndim
        widths[axis_dim] = (1 + shift, 1 - shift)
        widened = jnp.pad(member, widths)
        total = widened if total is None else total + widened
    return total


def fold_rim(values, axis_dim, depth_cells):
    length = values.shape[axis_dim] - 2 * depth_cells - 2
    interior = lax.slice_in_dim(values, depth_cells + 1, depth_cells + 1 + length, axis=axis_dim)
    lower_rim = lax.slice_in_dim(values, depth_cells - 1, depth_cells, axis=axis_dim)
    upper_rim = lax.slice_in_dim(
        values, depth_cells + 2 + length, depth_cells + 3 + length, axis=axis_dim
    )
    head = lax.slice_in_dim(interior, 0, 1, axis=axis_dim) + lower_rim
    middle = lax.slice_in_dim(interior, 1, length - 1, axis=axis_dim)
    tail = lax.slice_in_dim(interior, length - 1, length, axis=axis_dim) + upper_rim
    return jnp.concatenate([head, middle, tail], axis=axis_dim)


def shards(positions, grain_radii, film_liquid, pair_live, partner, rupture, volume):
    extent_x, extent_y, extent_z, grains = grain_radii.shape
    tile_count = extent_x * extent_y * extent_z
    slot_count = 27 * tile_count
    grain_state = jnp.concatenate([positions, grain_radii[None], film_liquid[None]], axis=0)
    border = padded(grain_state, (("gx", 1), ("gy", 2), ("gz", 3)), 1)
    anchor = jnp.repeat(grain_state.reshape(5, tile_count, grains).transpose(1, 0, 2), 27, axis=0)
    facing = []
    for along_x in (-1, 0, 1):
        for along_y in (-1, 0, 1):
            for along_z in (-1, 0, 1):
                start = (0, 1 + along_x, 1 + along_y, 1 + along_z, 0)
                limit = (
                    5,
                    1 + along_x + extent_x,
                    1 + along_y + extent_y,
                    1 + along_z + extent_z,
                    grains,
                )
                facing.append(lax.slice(border, start, limit))
    others = jnp.stack(facing, axis=4).reshape(5, slot_count, grains).transpose(1, 0, 2)
    centre = (jnp.arange(slot_count, dtype=jnp.int32) % 27 == 13).astype(jnp.float32)
    live_flags = pair_live.reshape(slot_count)
    pieces = (
        anchor,
        others,
        centre,
        live_flags.astype(jnp.float32),
        partner.reshape(slot_count, grains),
        rupture.reshape(slot_count, grains),
        volume.reshape(slot_count, grains),
    )
    block_span = 27 * block_tiles
    block_count = slot_count // block_span
    ranking = jnp.argsort(1 - live_flags, stable=True)
    packed = jax.tree.map(lambda member: member[ranking], pieces)
    blocked = jax.tree.map(
        lambda member: member.reshape((block_count, block_span) + member.shape[1:]), packed
    )
    needed = (jnp.sum(live_flags) + block_span - 1) // block_span
    empty = (
        jnp.zeros((block_count, block_span, 4, grains), jnp.float32),
        jnp.zeros((block_count, block_span, 4, grains), jnp.float32),
        jnp.zeros((block_count, block_span, grains), jnp.float32),
    )

    def advance(number, carry):
        piece = jax.tree.map(
            lambda member: lax.dynamic_index_in_dim(member, number, 0, keepdims=False), blocked
        )
        result = evaluate(piece)
        return jax.tree.map(
            lambda held, latest: lax.dynamic_update_index_in_dim(held, latest, number, 0),
            carry,
            result,
        )

    results = lax.fori_loop(0, needed, advance, empty)
    flat = jax.tree.map(lambda member: member.reshape((slot_count,) + member.shape[2:]), results)
    inverse = jnp.argsort(ranking)
    anchor_side, other_side, fresh = jax.tree.map(lambda member: member[inverse], flat)
    own_terms = jnp.sum(anchor_side.reshape(extent_x, extent_y, extent_z, 27, 4, grains), axis=3)
    far_terms = other_side.reshape(extent_x, extent_y, extent_z, 3, 3, 3, 4, grains)
    section_z = spread_three([far_terms[:, :, :, :, :, index] for index in range(3)], 2)
    section_y = spread_three([section_z[:, :, :, :, index] for index in range(3)], 1)
    section_x = spread_three([section_y[:, :, :, index] for index in range(3)], 0)
    gathered = section_x + jnp.pad(own_terms, ((1, 1), (1, 1), (1, 1), (0, 0), (0, 0)))
    totals = gathered.transpose(3, 0, 1, 2, 4)
    widened = padded(totals, (("gx", 1), ("gy", 2), ("gz", 3)), 2)
    folded = fold_rim(fold_rim(fold_rim(widened, 1, 2), 2, 2), 3, 2)
    forces = folded[:3]
    film_next = film_liquid + folded[3]
    volume_next = fresh.reshape(1, 1, 1, slot_count, grains)
    return (forces, film_next, volume_next)


def solution(mesh):
    return jax.shard_map(
        shards,
        mesh=mesh,
        in_specs=(
            P(None, "gx", "gy", "gz", None),
            P("gx", "gy", "gz", None),
            P("gx", "gy", "gz", None),
            P("gx", "gy", "gz", None),
            P("gx", "gy", "gz", None, None),
            P("gx", "gy", "gz", None, None),
            P("gx", "gy", "gz", None, None),
        ),
        out_specs=(
            P(None, "gx", "gy", "gz", None),
            P("gx", "gy", "gz", None),
            P("gx", "gy", "gz", None, None),
        ),
        check_vma=False,
    )
```

profile of v0, /device:TPU:169, one launch (start us, length us, event | category | flops | bytes accessed | tf_op | source)
XLA Modules:
  0.0 332.5 jit_solution(2404694382453337542)
XLA Ops:
  8.9 4.4 %sort.34 = (s32[864]{0:T(1024)}, s32[864]{0:T(1024)S(1)}) sort(s32[864]{0:T(1024)S(1)} %get-tuple-element.168, s32[864]{0:T(1024)S(1)} %iota.29), dimensions={0}, to_apply=%region_1.2 | sort | flops 8640 | bytes 13824 | tf_op jit(solution)/shard_map/jit(argsort)/sort | solution.py:136
  13.3 4.4 %sort.35 = (s32[864]{0:T(1024)}, s32[864]{0:T(1024)S(1)}) sort(s32[864]{0:T(1024)S(1)} %get-tuple-element.70, s32[864]{0:T(1024)S(1)} %iota.31), dimensions={0}, to_apply=%region_11.12 | sort | flops 8640 | bytes 13824 | tf_op jit(solution)/shard_map/jit(argsort)/sort | solution.py:161
  19.4 3.8 %collective-permute-start.2 = (f32[5,6,1,2,128]{4,3,2,1,0:T(2,128)S(1)}, f32[5,6,1,2,128]{4,3,2,1,0:T(2,128)S(1)}, u32[]{:S(2)}, u32[]{:S(2)}) collective-permute-start(f32[5,6,1,2,128]{4,3,2,1,0:T(2,128)S(1)} %get-tuple-element.240), channel_id=1, source_target_pairs={{0,4},{4,8},{8,12},{12,16},{16,20},{20,24},{24,28},{28,32},{32,36}... | collective-permute-start | bytes 92168 | tf_op jit(solution)/shard_map/ppermute | solution.py:18
  27.9 5.0 %gather_fusion = f32[864,5,128]{2,1,0:T(8,128)} fusion(f32[864,5,128]{2,1,0:T(8,128)} %bitcast.270, s32[1024]{0:T(1024)S(1)} %get-tuple-element.245), kind=kCustom, calls=%fused_computation | custom fusion | bytes 4427136 | tf_op jit(solution)/shard_map/gather | solution.py:137
  53.0 3.7 %collective-permute-done.5 = f32[5,6,6,1,128]{4,3,2,1,0:T(1,128)S(1)} collective-permute-done((f32[5,6,6,1,128]{4,3,2,1,0:T(1,128)S(1)}, f32[5,6,6,1,128]{4,3,2,1,0:T(1,128)S(1)}, u32[]{:S(2)}, u32[]{:S(2)}) %collective-permute-start.5) | collective-permute-done | bytes 92192 | tf_op jit(solution)/shard_map/ppermute | solution.py:20
  61.4 5.1 %gather_fusion.1 = f32[864,5,128]{2,1,0:T(8,128)} fusion(f32[864,5,128]{2,1,0:T(8,128)} %bitcast.271, s32[1024]{0:T(1024)S(1)} %get-tuple-element.245), kind=kCustom, calls=%fused_computation.1 | custom fusion | bytes 4427136 | tf_op jit(solution)/shard_map/gather | solution.py:137
  68.3 165.5 %while.14 = (s32[]{:T(128)}, f32[16,54,4,128]{3,2,1,0:T(4,128)S(1)}, f32[16,54,4,128]{3,2,1,0:T(4,128)}, f32[16,54,128]{2,0,1:T(8,128)S(1)}, s32[]{:T(128)}, /*i...) while((s32[]{:T(128)}, ...), condition=%wide.region_10.11_spmd, body=%wide.region_2.10_spmd.sunk | while | flops 124490296 | bytes 4750891 | solution.py:159
  70.4 4.0 %fusion.99 = f32[54,5,128]{2,1,0:T(8,128)S(1)} fusion(f32[54,5,128]{2,1,0:T(8,128)S(1)} %get-tuple-element.348, s32[54,128]{1,0:T(8,128)S(1)} %dynamic-slice_bitcast_fusion.6), kind=kOutput, calls=%fused_computation.33.clone.1 | convolution fusion | flops 53968896 | bytes 304128 | tf_op jit(solution)/shard_map/while/body/ncj,nij->nci/dot_general | solution.py:50
  76.2 10.4 %fusion.104 = (f32[54,128]{1,0:T(8,128)S(1)}, f32[54,128]{1,0:T(8,128)S(1)}, f32[54,128]{1,0:T(8,128)S(1)}, f32[54,128]{1,0:T(8,128)S(1)}, f32[54,128]{1,0:T(8,128)S(1)}, /*index=5*/f32[54,128]{1,0:T(8,128)S(1)}) fusion(f32[54,128]{1,0:T(8,128)S(1)} %bitcast.302, f32[54,128]{1,0:T(8,128)S(1)} %bitcast.298, f32[54]{0:T(128)S(1)} %fusion.100, ...), kind=kLoop, calls=%fused_computation.34.clone.1 | loop fusion | flops 26500608 | bytes 453040 | tf_op jit(solution)/shard_map/while/body/reduce_sum | solution.py:46
  87.0 3.8 %fusion.106 = f32[16,54,4,128]{3,2,1,0:T(4,128)} fusion(f32[16,54,4,128]{3,2,1,0:T(4,128)} %get-tuple-element.392, s32[]{:T(128)S(6)} %select_n.55, s32[54,128]{1,0:T(8,128)S(1)} %dynamic-slice_bitcast_fusion.6, f32[54,1,128]{2,1,0:T(1,128)S(1)} %broadcast.331, f32[54,1,128]{2,1,0:T(1,128)S(1)} %get-tuple-element.369, ...), kind=kOutput, calls=%fused_computation.44.clone.1 | convolution fusion | flops 43490304 | bytes 359428 | tf_op jit(solution)/shard_map/while/body/nci,nij->ncj/dot_general | solution.py:66
  94.0 4.0 %fusion.99 = f32[54,5,128]{2,1,0:T(8,128)S(1)} fusion(f32[54,5,128]{2,1,0:T(8,128)S(1)} %get-tuple-element.348, s32[54,128]{1,0:T(8,128)S(1)} %dynamic-slice_bitcast_fusion.6), kind=kOutput, calls=%fused_computation.33.clone.1 | convolution fusion | flops 53968896 | bytes 304128 | tf_op jit(solution)/shard_map/while/body/ncj,nij->nci/dot_general | solution.py:50
  99.8 10.4 %fusion.104 = (f32[54,128]{1,0:T(8,128)S(1)}, f32[54,128]{1,0:T(8,128)S(1)}, f32[54,128]{1,0:T(8,128)S(1)}, f32[54,128]{1,0:T(8,128)S(1)}, f32[54,128]{1,0:T(8,128)S(1)}, /*index=5*/f32[54,128]{1,0:T(8,128)S(1)}) fusion(f32[54,128]{1,0:T(8,128)S(1)} %bitcast.302, f32[54,128]{1,0:T(8,128)S(1)} %bitcast.298, f32[54]{0:T(128)S(1)} %fusion.100, ...), kind=kLoop, calls=%fused_computation.34.clone.1 | loop fusion | flops 26500608 | bytes 453040 | tf_op jit(solution)/shard_map/while/body/reduce_sum | solution.py:46
  110.6 3.8 %fusion.106 = f32[16,54,4,128]{3,2,1,0:T(4,128)} fusion(f32[16,54,4,128]{3,2,1,0:T(4,128)} %get-tuple-element.392, s32[]{:T(128)S(6)} %select_n.55, s32[54,128]{1,0:T(8,128)S(1)} %dynamic-slice_bitcast_fusion.6, f32[54,1,128]{2,1,0:T(1,128)S(1)} %broadcast.331, f32[54,1,128]{2,1,0:T(1,128)S(1)} %get-tuple-element.369, ...), kind=kOutput, calls=%fused_computation.44.clone.1 | convolution fusion | flops 43490304 | bytes 359428 | tf_op jit(solution)/shard_map/while/body/nci,nij->ncj/dot_general | solution.py:66
  117.6 4.0 %fusion.99 = f32[54,5,128]{2,1,0:T(8,128)S(1)} fusion(f32[54,5,128]{2,1,0:T(8,128)S(1)} %get-tuple-element.348, s32[54,128]{1,0:T(8,128)S(1)} %dynamic-slice_bitcast_fusion.6), kind=kOutput, calls=%fused_computation.33.clone.1 | convolution fusion | flops 53968896 | bytes 304128 | tf_op jit(solution)/shard_map/while/body/ncj,nij->nci/dot_general | solution.py:50
  123.4 10.4 %fusion.104 = (f32[54,128]{1,0:T(8,128)S(1)}, f32[54,128]{1,0:T(8,128)S(1)}, f32[54,128]{1,0:T(8,128)S(1)}, f32[54,128]{1,0:T(8,128)S(1)}, f32[54,128]{1,0:T(8,128)S(1)}, /*index=5*/f32[54,128]{1,0:T(8,128)S(1)}) fusion(f32[54,128]{1,0:T(8,128)S(1)} %bitcast.302, f32[54,128]{1,0:T(8,128)S(1)} %bitcast.298, f32[54]{0:T(128)S(1)} %fusion.100, ...), kind=kLoop, calls=%fused_computation.34.clone.1 | loop fusion | flops 26500608 | bytes 453040 | tf_op jit(solution)/shard_map/while/body/reduce_sum | solution.py:46
  134.2 3.8 %fusion.106 = f32[16,54,4,128]{3,2,1,0:T(4,128)} fusion(f32[16,54,4,128]{3,2,1,0:T(4,128)} %get-tuple-element.392, s32[]{:T(128)S(6)} %select_n.55, s32[54,128]{1,0:T(8,128)S(1)} %dynamic-slice_bitcast_fusion.6, f32[54,1,128]{2,1,0:T(1,128)S(1)} %broadcast.331, f32[54,1,128]{2,1,0:T(1,128)S(1)} %get-tuple-element.369, ...), kind=kOutput, calls=%fused_computation.44.clone.1 | convolution fusion | flops 43490304 | bytes 359428 | tf_op jit(solution)/shard_map/while/body/nci,nij->ncj/dot_general | solution.py:66
  141.2 4.0 %fusion.99 = f32[54,5,128]{2,1,0:T(8,128)S(1)} fusion(f32[54,5,128]{2,1,0:T(8,128)S(1)} %get-tuple-element.348, s32[54,128]{1,0:T(8,128)S(1)} %dynamic-slice_bitcast_fusion.6), kind=kOutput, calls=%fused_computation.33.clone.1 | convolution fusion | flops 53968896 | bytes 304128 | tf_op jit(solution)/shard_map/while/body/ncj,nij->nci/dot_general | solution.py:50
  147.0 10.4 %fusion.104 = (f32[54,128]{1,0:T(8,128)S(1)}, f32[54,128]{1,0:T(8,128)S(1)}, f32[54,128]{1,0:T(8,128)S(1)}, f32[54,128]{1,0:T(8,128)S(1)}, f32[54,128]{1,0:T(8,128)S(1)}, /*index=5*/f32[54,128]{1,0:T(8,128)S(1)}) fusion(f32[54,128]{1,0:T(8,128)S(1)} %bitcast.302, f32[54,128]{1,0:T(8,128)S(1)} %bitcast.298, f32[54]{0:T(128)S(1)} %fusion.100, ...), kind=kLoop, calls=%fused_computation.34.clone.1 | loop fusion | flops 26500608 | bytes 453040 | tf_op jit(solution)/shard_map/while/body/reduce_sum | solution.py:46
  157.9 3.8 %fusion.106 = f32[16,54,4,128]{3,2,1,0:T(4,128)} fusion(f32[16,54,4,128]{3,2,1,0:T(4,128)} %get-tuple-element.392, s32[]{:T(128)S(6)} %select_n.55, s32[54,128]{1,0:T(8,128)S(1)} %dynamic-slice_bitcast_fusion.6, f32[54,1,128]{2,1,0:T(1,128)S(1)} %broadcast.331, f32[54,1,128]{2,1,0:T(1,128)S(1)} %get-tuple-element.369, ...), kind=kOutput, calls=%fused_computation.44.clone.1 | convolution fusion | flops 43490304 | bytes 359428 | tf_op jit(solution)/shard_map/while/body/nci,nij->ncj/dot_general | solution.py:66
  164.8 4.0 %fusion.99 = f32[54,5,128]{2,1,0:T(8,128)S(1)} fusion(f32[54,5,128]{2,1,0:T(8,128)S(1)} %get-tuple-element.348, s32[54,128]{1,0:T(8,128)S(1)} %dynamic-slice_bitcast_fusion.6), kind=kOutput, calls=%fused_computation.33.clone.1 | convolution fusion | flops 53968896 | bytes 304128 | tf_op jit(solution)/shard_map/while/body/ncj,nij->nci/dot_general | solution.py:50
  170.6 10.4 %fusion.104 = (f32[54,128]{1,0:T(8,128)S(1)}, f32[54,128]{1,0:T(8,128)S(1)}, f32[54,128]{1,0:T(8,128)S(1)}, f32[54,128]{1,0:T(8,128)S(1)}, f32[54,128]{1,0:T(8,128)S(1)}, /*index=5*/f32[54,128]{1,0:T(8,128)S(1)}) fusion(f32[54,128]{1,0:T(8,128)S(1)} %bitcast.302, f32[54,128]{1,0:T(8,128)S(1)} %bitcast.298, f32[54]{0:T(128)S(1)} %fusion.100, ...), kind=kLoop, calls=%fused_computation.34.clone.1 | loop fusion | flops 26500608 | bytes 453040 | tf_op jit(solution)/shard_map/while/body/reduce_sum | solution.py:46
  181.5 3.8 %fusion.106 = f32[16,54,4,128]{3,2,1,0:T(4,128)} fusion(f32[16,54,4,128]{3,2,1,0:T(4,128)} %get-tuple-element.392, s32[]{:T(128)S(6)} %select_n.55, s32[54,128]{1,0:T(8,128)S(1)} %dynamic-slice_bitcast_fusion.6, f32[54,1,128]{2,1,0:T(1,128)S(1)} %broadcast.331, f32[54,1,128]{2,1,0:T(1,128)S(1)} %get-tuple-element.369, ...), kind=kOutput, calls=%fused_computation.44.clone.1 | convolution fusion | flops 43490304 | bytes 359428 | tf_op jit(solution)/shard_map/while/body/nci,nij->ncj/dot_general | solution.py:66
  188.4 4.0 %fusion.99 = f32[54,5,128]{2,1,0:T(8,128)S(1)} fusion(f32[54,5,128]{2,1,0:T(8,128)S(1)} %get-tuple-element.348, s32[54,128]{1,0:T(8,128)S(1)} %dynamic-slice_bitcast_fusion.6), kind=kOutput, calls=%fused_computation.33.clone.1 | convolution fusion | flops 53968896 | bytes 304128 | tf_op jit(solution)/shard_map/while/body/ncj,nij->nci/dot_general | solution.py:50
  194.3 10.4 %fusion.104 = (f32[54,128]{1,0:T(8,128)S(1)}, f32[54,128]{1,0:T(8,128)S(1)}, f32[54,128]{1,0:T(8,128)S(1)}, f32[54,128]{1,0:T(8,128)S(1)}, f32[54,128]{1,0:T(8,128)S(1)}, /*index=5*/f32[54,128]{1,0:T(8,128)S(1)}) fusion(f32[54,128]{1,0:T(8,128)S(1)} %bitcast.302, f32[54,128]{1,0:T(8,128)S(1)} %bitcast.298, f32[54]{0:T(128)S(1)} %fusion.100, ...), kind=kLoop, calls=%fused_computation.34.clone.1 | loop fusion | flops 26500608 | bytes 453040 | tf_op jit(solution)/shard_map/while/body/reduce_sum | solution.py:46
  205.1 3.8 %fusion.106 = f32[16,54,4,128]{3,2,1,0:T(4,128)} fusion(f32[16,54,4,128]{3,2,1,0:T(4,128)} %get-tuple-element.392, s32[]{:T(128)S(6)} %select_n.55, s32[54,128]{1,0:T(8,128)S(1)} %dynamic-slice_bitcast_fusion.6, f32[54,1,128]{2,1,0:T(1,128)S(1)} %broadcast.331, f32[54,1,128]{2,1,0:T(1,128)S(1)} %get-tuple-element.369, ...), kind=kOutput, calls=%fused_computation.44.clone.1 | convolution fusion | flops 43490304 | bytes 359428 | tf_op jit(solution)/shard_map/while/body/nci,nij->ncj/dot_general | solution.py:66
  212.1 4.0 %fusion.99 = f32[54,5,128]{2,1,0:T(8,128)S(1)} fusion(f32[54,5,128]{2,1,0:T(8,128)S(1)} %get-tuple-element.348, s32[54,128]{1,0:T(8,128)S(1)} %dynamic-slice_bitcast_fusion.6), kind=kOutput, calls=%fused_computation.33.clone.1 | convolution fusion | flops 53968896 | bytes 304128 | tf_op jit(solution)/shard_map/while/body/ncj,nij->nci/dot_general | solution.py:50
  217.9 10.4 %fusion.104 = (f32[54,128]{1,0:T(8,128)S(1)}, f32[54,128]{1,0:T(8,128)S(1)}, f32[54,128]{1,0:T(8,128)S(1)}, f32[54,128]{1,0:T(8,128)S(1)}, f32[54,128]{1,0:T(8,128)S(1)}, /*index=5*/f32[54,128]{1,0:T(8,128)S(1)}) fusion(f32[54,128]{1,0:T(8,128)S(1)} %bitcast.302, f32[54,128]{1,0:T(8,128)S(1)} %bitcast.298, f32[54]{0:T(128)S(1)} %fusion.100, ...), kind=kLoop, calls=%fused_computation.34.clone.1 | loop fusion | flops 26500608 | bytes 453040 | tf_op jit(solution)/shard_map/while/body/reduce_sum | solution.py:46
  228.7 3.8 %fusion.106 = f32[16,54,4,128]{3,2,1,0:T(4,128)} fusion(f32[16,54,4,128]{3,2,1,0:T(4,128)} %get-tuple-element.392, s32[]{:T(128)S(6)} %select_n.55, s32[54,128]{1,0:T(8,128)S(1)} %dynamic-slice_bitcast_fusion.6, f32[54,1,128]{2,1,0:T(1,128)S(1)} %broadcast.331, f32[54,1,128]{2,1,0:T(1,128)S(1)} %get-tuple-element.369, ...), kind=kOutput, calls=%fused_computation.44.clone.1 | convolution fusion | flops 43490304 | bytes 359428 | tf_op jit(solution)/shard_map/while/body/nci,nij->ncj/dot_general | solution.py:66
  240.9 4.0 %gather_fusion.8 = f32[864,4,128]{2,1,0:T(4,128)} fusion(f32[864,4,128]{2,1,0:T(4,128)S(1)} %bitcast.273, s32[1024]{0:T(1024)S(1)} %get-tuple-element.244), kind=kCustom, calls=%fused_computation.8 | custom fusion | bytes 3542400 | tf_op jit(solution)/shard_map/gather | solution.py:162
  256.0 7.2 %collective-permute-start.9 = (f32[4,10,2,4,128]{4,0,3,2,1:T(4,128)S(1)}, f32[4,10,2,4,128]{4,0,3,2,1:T(4,128)S(1)}, u32[]{:S(2)}, u32[]{:S(2)}) collective-permute-start(f32[4,10,2,4,128]{4,0,3,2,1:T(4,128)S(1)} %get-tuple-element.229), channel_id=1, source_target_pairs={{4,0},{8,4},{12,8},{16,12},{20,16},{24,20},{28,24},{32,28},{36,32}... | collective-permute-start | bytes 491528 | tf_op jit(solution)/shard_map/ppermute | solution.py:20
  265.4 54.7 %collective-permute-start.10 = (f32[4,10,10,2,128]{4,0,3,2,1:T(4,128)}, f32[4,10,10,2,128]{4,0,3,2,1:T(4,128)S(1)}, u32[]{:S(2)}, u32[]{:S(2)}) collective-permute-start(f32[4,10,10,2,128]{4,0,3,2,1:T(4,128)} %get-tuple-element.221), channel_id=1, source_target_pairs={{0,1},{1,2},{2,3},{4,5},{5,6},{6,7},{8,9},{9,10},{10,11},{12,13},{... | collective-permute-start | bytes 1228808 | tf_op jit(solution)/shard_map/ppermute | solution.py:18
  326.7 4.0 %collective-permute-done.11 = f32[4,10,10,2,128]{4,0,3,2,1:T(4,128)S(1)} collective-permute-done((f32[4,10,10,2,128]{4,0,3,2,1:T(4,128)}, f32[4,10,10,2,128]{4,0,3,2,1:T(4,128)S(1)}, u32[]{:S(2)}, u32[]{:S(2)}) %collective-permute-start.11) | collective-permute-done | bytes 409632 | tf_op jit(solution)/shard_map/ppermute | solution.py:20
  (338 shorter events, 105.2 us)
Async XLA Ops:
  0.6 32.3 %copy-start = (s32[1,1,1,864,128]{4,3,2,1,0:T(8,128)S(1)}, s32[1,1,1,864,128]{4,3,2,1,0:T(8,128)}, u32[]{:S(2)}) copy-start(s32[1,1,1,864,128]{4,3,2,1,0:T(8,128)} %param.14) | copy-start | bytes 1327108
  1.6 16.9 %collective-permute-start = (f32[5,1,4,2,128]{4,3,2,1,0:T(2,128)S(1)}, f32[5,1,4,2,128]{4,3,2,1,0:T(2,128)S(1)}, u32[]{:S(2)}, u32[]{:S(2)}) collective-permute-start(f32[5,1,4,2,128]{4,3,2,1,0:T(2,128)S(1)} %get-tuple-element.242), channel_id=1, source_target_pairs={{0,64},{64,128},{128,192},{1,65},{65,129},{129,193},{2,66},{66,130... | collective-permute-start | bytes 61448 | tf_op jit(solution)/shard_map/ppermute | solution.py:18
  4.8 13.7 %collective-permute-start.1 = (f32[5,1,4,2,128]{4,3,2,1,0:T(2,128)S(1)}, f32[5,1,4,2,128]{4,3,2,1,0:T(2,128)S(1)}, u32[]{:S(2)}, u32[]{:S(2)}) collective-permute-start(f32[5,1,4,2,128]{4,3,2,1,0:T(2,128)S(1)} %get-tuple-element.243), channel_id=1, source_target_pairs={{64,0},{128,64},{192,128},{65,1},{129,65},{193,129},{66,2},{130,66... | collective-permute-start | bytes 61448 | tf_op jit(solution)/shard_map/ppermute | solution.py:20
  19.4 28.6 %collective-permute-start.2 = (f32[5,6,1,2,128]{4,3,2,1,0:T(2,128)S(1)}, f32[5,6,1,2,128]{4,3,2,1,0:T(2,128)S(1)}, u32[]{:S(2)}, u32[]{:S(2)}) collective-permute-start(f32[5,6,1,2,128]{4,3,2,1,0:T(2,128)S(1)} %get-tuple-element.240), channel_id=1, source_target_pairs={{0,4},{4,8},{8,12},{12,16},{16,20},{20,24},{24,28},{28,32},{32,36}... | collective-permute-start | bytes 92168 | tf_op jit(solution)/shard_map/ppermute | solution.py:18
  23.2 24.9 %collective-permute-start.3 = (f32[5,6,1,2,128]{4,3,2,1,0:T(2,128)S(1)}, f32[5,6,1,2,128]{4,3,2,1,0:T(2,128)S(1)}, u32[]{:S(2)}, u32[]{:S(2)}) collective-permute-start(f32[5,6,1,2,128]{4,3,2,1,0:T(2,128)S(1)} %get-tuple-element.241), channel_id=1, source_target_pairs={{4,0},{8,4},{12,8},{16,12},{20,16},{24,20},{28,24},{32,28},{36,32}... | collective-permute-start | bytes 92168 | tf_op jit(solution)/shard_map/ppermute | solution.py:20
  32.9 2.0 copy-start.1
  34.9 2.8 copy-start.2
  44.1 3.9 %copy-start.5 = (f32[3,4,4,2,128]{4,3,2,1,0:T(2,128)S(1)}, f32[3,4,4,2,128]{4,3,2,1,0:T(2,128)}, u32[]{:S(2)}) copy-start(f32[3,4,4,2,128]{4,3,2,1,0:T(2,128)} %param.9) | copy-start | bytes 147460
  44.1 3.9 %copy-start.6 = (f32[4,4,2,128]{3,2,1,0:T(2,128)S(1)}, f32[4,4,2,128]{3,2,1,0:T(2,128)}, u32[]{:S(2)}) copy-start(f32[4,4,2,128]{3,2,1,0:T(2,128)} %param.11) | copy-start | bytes 49156
  44.1 3.9 %copy-start.7 = (f32[4,4,2,128]{3,2,1,0:T(2,128)S(1)}, f32[4,4,2,128]{3,2,1,0:T(2,128)}, u32[]{:S(2)}) copy-start(f32[4,4,2,128]{3,2,1,0:T(2,128)} %param.10) | copy-start | bytes 49156
  48.3 4.7 %collective-permute-start.4 = (f32[5,6,6,1,128]{4,3,2,1,0:T(1,128)S(1)}, f32[5,6,6,1,128]{4,3,2,1,0:T(1,128)S(1)}, u32[]{:S(2)}, u32[]{:S(2)}) collective-permute-start(f32[5,6,6,1,128]{4,3,2,1,0:T(1,128)S(1)} %get-tuple-element.237), channel_id=1, source_target_pairs={{0,1},{1,2},{2,3},{4,5},{5,6},{6,7},{8,9},{9,10},{10,11},{12,13},{... | collective-permute-start | bytes 276488 | tf_op jit(solution)/shard_map/ppermute | solution.py:18
  51.4 5.3 %collective-permute-start.5 = (f32[5,6,6,1,128]{4,3,2,1,0:T(1,128)S(1)}, f32[5,6,6,1,128]{4,3,2,1,0:T(1,128)S(1)}, u32[]{:S(2)}, u32[]{:S(2)}) collective-permute-start(f32[5,6,6,1,128]{4,3,2,1,0:T(1,128)S(1)} %get-tuple-element.236), channel_id=1, source_target_pairs={{1,0},{2,1},{3,2},{5,4},{6,5},{7,6},{9,8},{10,9},{11,10},{13,12},{... | collective-permute-start | bytes 276488 | tf_op jit(solution)/shard_map/ppermute | solution.py:20
  233.8 1.2 copy-start.3
  239.4 1.5 copy-start.4
  246.7 5.4 %collective-permute-start.6 = (f32[4,2,6,4,128]{4,0,3,2,1:T(4,128)S(1)}, f32[4,2,6,4,128]{4,0,3,2,1:T(4,128)S(1)}, u32[]{:S(2)}, u32[]{:S(2)}) collective-permute-start(f32[4,2,6,4,128]{4,0,3,2,1:T(4,128)S(1)} %get-tuple-element.230), channel_id=1, source_target_pairs={{0,64},{64,128},{128,192},{1,65},{65,129},{129,193},{2,66},{66,130... | collective-permute-start | bytes 294920 | tf_op jit(solution)/shard_map/ppermute | solution.py:18
  248.6 5.4 %collective-permute-start.7 = (f32[4,2,6,4,128]{4,0,3,2,1:T(4,128)S(1)}, f32[4,2,6,4,128]{4,0,3,2,1:T(4,128)S(1)}, u32[]{:S(2)}, u32[]{:S(2)}) collective-permute-start(f32[4,2,6,4,128]{4,0,3,2,1:T(4,128)S(1)} %get-tuple-element.231), channel_id=1, source_target_pairs={{64,0},{128,64},{192,128},{65,1},{129,65},{193,129},{66,2},{130,66... | collective-permute-start | bytes 294920 | tf_op jit(solution)/shard_map/ppermute | solution.py:20
  254.0 9.1 %collective-permute-start.8 = (f32[4,10,2,4,128]{4,0,3,2,1:T(4,128)S(1)}, f32[4,10,2,4,128]{4,0,3,2,1:T(4,128)S(1)}, u32[]{:S(2)}, u32[]{:S(2)}) collective-permute-start(f32[4,10,2,4,128]{4,0,3,2,1:T(4,128)S(1)} %get-tuple-element.228), channel_id=1, source_target_pairs={{0,4},{4,8},{8,12},{12,16},{16,20},{20,24},{24,28},{28,32},{32,36}... | collective-permute-start | bytes 491528 | tf_op jit(solution)/shard_map/ppermute | solution.py:18
  256.0 8.2 %collective-permute-start.9 = (f32[4,10,2,4,128]{4,0,3,2,1:T(4,128)S(1)}, f32[4,10,2,4,128]{4,0,3,2,1:T(4,128)S(1)}, u32[]{:S(2)}, u32[]{:S(2)}) collective-permute-start(f32[4,10,2,4,128]{4,0,3,2,1:T(4,128)S(1)} %get-tuple-element.229), channel_id=1, source_target_pairs={{4,0},{8,4},{12,8},{16,12},{20,16},{24,20},{28,24},{32,28},{36,32}... | collective-permute-start | bytes 491528 | tf_op jit(solution)/shard_map/ppermute | solution.py:20
  265.4 61.3 %collective-permute-start.10 = (f32[4,10,10,2,128]{4,0,3,2,1:T(4,128)}, f32[4,10,10,2,128]{4,0,3,2,1:T(4,128)S(1)}, u32[]{:S(2)}, u32[]{:S(2)}) collective-permute-start(f32[4,10,10,2,128]{4,0,3,2,1:T(4,128)} %get-tuple-element.221), channel_id=1, source_target_pairs={{0,1},{1,2},{2,3},{4,5},{5,6},{6,7},{8,9},{9,10},{10,11},{12,13},{... | collective-permute-start | bytes 1228808 | tf_op jit(solution)/shard_map/ppermute | solution.py:18
  320.1 10.7 %collective-permute-start.11 = (f32[4,10,10,2,128]{4,0,3,2,1:T(4,128)}, f32[4,10,10,2,128]{4,0,3,2,1:T(4,128)S(1)}, u32[]{:S(2)}, u32[]{:S(2)}) collective-permute-start(f32[4,10,10,2,128]{4,0,3,2,1:T(4,128)} %get-tuple-element.222), channel_id=1, source_target_pairs={{1,0},{2,1},{3,2},{5,4},{6,5},{7,6},{9,8},{10,9},{11,10},{13,12},{... | collective-permute-start | bytes 1228808 | tf_op jit(solution)/shard_map/ppermute | solution.py:20
where the time goes:
time: 335 us; the launch traced here: 333 us
  other arithmetic  111 us (33%)
  starting transfers between devices  85.7 us (26%)
  local copies, waits for them, and re-layouts  63.8 us (19%)
  matrix products  54.4 us (16%)
  waiting for transfers between devices  13.3 us (4%)
    reduce_sum x7, other arithmetic, evaluate(): jnp.sum(member, axis=1)  72.9 us
    ppermute x6, starting transfers between devices, padded(): lax.ppermute(tail, axis, [(i, (i + 1) % count) for i in range(ends)])  68.6 us
    dot_general x7, matrix products, evaluate(): jnp.einsum('ncj,nij->nci', others, choose, precision=lax.Precision.HIGHEST)  27.7 us
    dot_general x7, matrix products, evaluate(): jnp.einsum('nci,nij->ncj', jnp.concatenate([bridge_force, liquid_other[:,...  26.7 us
    gather x7, local copies, waits for them, and re-layouts, shards(): packed = jax.tree.map(lambda member: member[ranking], pieces)  23.1 us
    ppermute x6, starting transfers between devices, padded(): lax.ppermute(head, axis, [((i + 1) % count, i) for i in range(ends)])  17.1 us
    ppermute x6, waiting for transfers between devices, padded(): lax.ppermute(head, axis, [((i + 1) % count, i) for i in range(ends)])  10.7 us
    gather x3, local copies, waits for them, and re-layouts, shards(): member[inverse]  10.4 us
  transfers between devices with their start and end apart: 12, of which 7 were waited for; matrix products, arithmetic and copies ran while one was open for 11% of the time, Pallas kernels for 0%

commit v1 on v0

v1 whole, which is shorter than its diff:
```python
import functools

import jax
import jax.numpy as jnp
import numpy as np
from jax import lax
from jax.experimental import pallas as pl
from jax.experimental.pallas import tpu as pltpu
from jax.sharding import PartitionSpec as P

ABSORB = 0.02
BX, BY, BZ = 4, 4, 2
TILES = BX * BY * BZ
SLOTS = 27 * TILES
G = 128
Z_ROWS = 16 * 32
Y_ROWS = 8 * 32 + 8 * 16
X_ROWS = 8 * 32 + 4 * 16 + 8 * 16 + 4 * 8
Z_AT = 0
Y_AT = 2 * Z_ROWS
X_AT = Y_AT + 2 * Y_ROWS
ZERO_AT = X_AT + 2 * X_ROWS
HALO_ROWS = ZERO_AT + 8
BATCH = 32
OFFSETS = [(i, j, k) for i in (-1, 0, 1) for j in (-1, 0, 1) for k in (-1, 0, 1)]


def tile_number(x, y, z):
    return (x * BY + y) * BZ + z


def code(e):
    return 9 * (e[0] + 1) + 3 * (e[1] + 1) + e[2] + 1


def inside(x, y, z):
    return 0 <= x < BX and 0 <= y < BY and 0 <= z < BZ


def halo_block(x, y, z):
    side = lambda v: 0 if v < 0 else 1
    ox, oy, oz = not 0 <= x < BX, not 0 <= y < BY, not 0 <= z < BZ
    if ox:
        base = X_AT + side(x) * X_ROWS
        if oy and oz:
            return base + 448 + (side(y) * 2 + side(z)) * 8, 1
        if oy:
            return base + 256 + (side(y) * 2 + z) * 16, 3
        if oz:
            return base + 320 + (side(z) * 4 + y) * 16, 3
        return base + (y * 2 + z) * 32, 9
    if oy:
        base = Y_AT + side(y) * Y_ROWS
        if oz:
            return base + 256 + (side(z) * 4 + x) * 16, 3
        return base + (x * 2 + z) * 32, 9
    return Z_AT + side(z) * Z_ROWS + (x * 4 + y) * 32, 9


def halo_slot(x, y, z, e):
    base, count = halo_block(x, y, z)
    free = [v + 1 for v, c, n in zip(e, (x, y, z), (BX, BY, BZ)) if 0 <= c < n]
    k = 0
    for v in free:
        k = 3 * k + v
    return base + 5 + k, base + 5 + count + k, base + 5 + 2 * count + k


def pairs():
    for x in range(BX):
        for y in range(BY):
            for z in range(BZ):
                for e in OFFSETS:
                    yield (x, y, z), e, (x + e[0], y + e[1], z + e[2])


def pad(rows, multiple, dummy):
    rows = list(rows)
    while len(rows) % multiple:
        rows.append(dummy)
    return rows


def bridge_tables():
    inner, outward, inward = [], [], []
    for t, e, b in pairs():
        own = 8 * tile_number(*t)
        s = 27 * tile_number(*t) + code(e)
        if inside(*b):
            inner.append((own, 8 * tile_number(*b), s, s, s))
        else:
            back = tuple(-v for v in e)
            outward.append((own, halo_block(*b)[0], s, s, s))
            inward.append((halo_block(*b)[0], own) + halo_slot(*b, back))
    return inner, outward, inward


def contact_class(e):
    kinds = sum(abs(v) for v in e)
    if kinds == 0:
        return 3
    if kinds > 1:
        return 0
    return 1 if e[0] else 2


CHUNKS = (1, 2, 4, 16)
UNROLL = (16, 8, 4, 2)


def contact_tables(halo):
    out = [[], [], [], []]
    for t, e, b in pairs():
        own = 8 * tile_number(*t)
        s = 27 * tile_number(*t) + code(e)
        back = tuple(-v for v in e)
        kind = contact_class(e)
        if inside(*b):
            s2 = 27 * tile_number(*b) + code(back)
            if not halo:
                out[kind].append((own, 8 * tile_number(*b), s, s2, s2))
        elif halo:
            _, ret, rel = halo_slot(*b, back)
            out[kind].append((own, halo_block(*b)[0], s, ret, rel))
    return out


def flat(rows):
    return np.asarray(rows, np.int32).reshape(-1)


def row(ref, at):
    return ref[pl.ds(at, 1), :]


def block(ref, at):
    return ref[pl.ds(pl.multiple_of(at, 8), 8), :]


def run_bridges(count, tab, a_ref, b_ref, p_ref, q_ref, l_ref, scr, acc_a, acc_b, next_ref):
    m_ref, a_scr, q_scr, l_scr, f_ref, g_ref = scr

    def body(i, carry):
        at = []
        for j in range(BATCH):
            o = (i * BATCH + j) * 5
            at.append([tab[o + k] for k in range(5)])
        partner = []
        for j in range(BATCH):
            a, b, p, q, l = at[j]
            idx = row(p_ref, p).astype(jnp.int32)
            m_ref[8 * j : 8 * j + 8, :] = jnp.take_along_axis(
                block(b_ref, b), jnp.broadcast_to(idx, (8, G)), axis=1
            )
            a_scr[8 * j : 8 * j + 8, :] = block(a_ref, a)
            q_scr[j : j + 1, :] = row(q_ref, q)
            l_scr[j : j + 1, :] = row(l_ref, l)
        for g in range(BATCH // 8):
            near = [m_ref[pl.ds(64 * g + c, 8, stride=8), :] for c in range(5)]
            own = [a_scr[pl.ds(64 * g + c, 8, stride=8), :] for c in range(5)]
            held = q_scr[8 * g : 8 * g + 8, :]
            half = 0.5 * l_scr[8 * g : 8 * g + 8, :]
            gap = [own[c] - near[c] for c in range(3)]
            squares = gap[0] * gap[0] + gap[1] * gap[1] + gap[2] * gap[2]
            inverse = lax.rsqrt(squares)
            spacing = squares * inverse
            radius_sum = own[3] + near[3]
            harmonic = 2.0 * own[3] * near[3] / radius_sum
            scaled = (
                jnp.maximum(spacing - radius_sum, 0.0) * harmonic * lax.rsqrt(harmonic * held)
            )
            intact = held > 0.0
            tension = harmonic * inverse / (1.0 + 1.05 * scaled + 2.5 * scaled * scaled)
            tension = jnp.where(intact, tension, 0.0)
            absorb = jnp.where(intact, ABSORB, 0.0)
            force = [tension * gap[c] for c in range(3)]
            if acc_b is not None:
                for c, value in enumerate(force + [half - absorb * near[4]]):
                    high = value.astype(jnp.bfloat16).astype(jnp.float32)
                    f_ref[pl.ds(64 * g + c, 8, stride=8), :] = high
                    f_ref[pl.ds(64 * g + 4 + c, 8, stride=8), :] = value - high
            if acc_a is not None:
                for c in range(3):
                    g_ref[pl.ds(64 * g + c, 8, stride=8), :] = -force[c]
                g_ref[pl.ds(64 * g + 3, 8, stride=8), :] = half - absorb * own[4]
                g_ref[pl.ds(64 * g + 4, 8, stride=8), :] = jnp.where(
                    intact, held + ABSORB * (own[4] + near[4]), 0.0
                )
        if acc_a is not None:
            for j in range(BATCH):
                a, b, p, q, l = at[j]
                here = pl.ds(pl.multiple_of(a, 8), 8)
                acc_a[here, :] = acc_a[here, :] + g_ref[8 * j : 8 * j + 8, :]
                next_ref[pl.ds(p, 1), :] = g_ref[8 * j + 4 : 8 * j + 5, :]
        if acc_b is not None:
            sub = lax.broadcasted_iota(jnp.int32, (G, G), 0)
            for j in range(BATCH):
                a, b, p, q, l = at[j]
                idx = row(p_ref, p).astype(jnp.int32)
                choose = (sub == idx).astype(jnp.bfloat16)
                landed = lax.dot_general(
                    f_ref[8 * j : 8 * j + 8, :].astype(jnp.bfloat16),
                    choose,
                    (((1,), (1,)), ((), ())),
                    preferred_element_type=jnp.float32,
                )
                here = pl.ds(pl.multiple_of(b, 8), 8)
                acc_b[here, :] = acc_b[here, :] + landed
        return carry

    lax.fori_loop(0, count // BATCH, body, 0)


def chunk_force(key, base, other, target):
    sub = lax.broadcasted_iota(jnp.int32, (8, G), 0).astype(jnp.float32) + base
    chosen = key == sub
    rows = [
        jnp.sum(jnp.where(chosen, other[c], 0.0), axis=1, keepdims=True) for c in range(4)
    ]
    radius = jnp.where(rows[3] > 0.0, rows[3], -1000.0)
    delta = [target[c] - rows[c] for c in range(3)]
    squares = delta[0] * delta[0] + delta[1] * delta[1] + delta[2] * delta[2]
    squares = jnp.maximum(squares, 1e-6)
    inverse = lax.rsqrt(squares)
    reach = target[3] + radius
    overlap = jnp.maximum(reach - squares * inverse, 0.0)
    weight = target[3] * radius * overlap
    push = overlap * inverse * weight * lax.rsqrt(jnp.maximum(weight * reach, 1e-30))
    return [push * delta[c] for c in range(3)]


def run_contacts(sizes, tab, t_ref, n_ref, q_ref, l_ref, nq_ref, nl_ref, low, high, mark, keys, acc):
    total = sum(sizes)
    wide = lax.broadcasted_iota(jnp.int32, (8, G), 0)

    def near(i, carry):
        for u in range(16):
            j = i * 16 + u
            t, n, s, nq, nl = [tab[j * 5 + k] for k in range(5)]
            live = row(q_ref, s) + row(l_ref, s) + row(nq_ref, nq) + row(nl_ref, nl) > 0.0
            value = block(n_ref, n)
            top = block(high, t)
            gap = jnp.maximum(jnp.maximum(block(low, t) - value, value - top), 0.0)
            gap = jnp.where(wide < 3, gap * gap, 0.0)
            distance = jnp.sum(gap, axis=0, keepdims=True)
            limit = value[3:4, :] + top[3:4, :] + 0.001
            mark[pl.ds(j, 1), :] = jnp.where(
                live & (distance <= limit * limit), 1.0, 0.0
            )
        return carry

    lax.fori_loop(0, total // 16, near, 0)
    lane = lax.broadcasted_iota(jnp.int32, (G, G), 1)
    sub = lax.broadcasted_iota(jnp.int32, (G, G), 0)
    upper = (sub <= lane).astype(jnp.bfloat16)
    start = 0
    crowded = []
    for kind, size in enumerate(sizes):
        if not size:
            continue
        if kind == 3:
            keys[start : start + size, :] = lax.broadcasted_iota(
                jnp.int32, (size, G), 1
            ).astype(jnp.float32)
        else:
            held = mark[start : start + size, :]
            rank = jnp.dot(
                held.astype(jnp.bfloat16), upper, preferred_element_type=jnp.float32
            )
            keys[start : start + size, :] = jnp.where(held > 0.0, rank - 1.0, -1.0)
            crowded.append((kind, start, size, jnp.max(rank) > 8.0 * CHUNKS[kind]))
        start += size

    def job(j, chunk_list):
        t, n = tab[j * 5], tab[j * 5 + 1]
        target = block(t_ref, t)
        other = block(n_ref, n)
        target = [target[c : c + 1, :] for c in range(4)]
        other = [other[c : c + 1, :] for c in range(4)]
        key = row(keys, j)
        force = None
        for base in chunk_list:
            part = chunk_force(key, base, other, target)
            force = part if force is None else [x + y for x, y in zip(force, part)]
        for c in range(3):
            here = pl.ds(pl.multiple_of(t * 3 + 8 * c, 8), 8)
            acc[here, :] = acc[here, :] + force[c]

    start = 0
    for kind, size in enumerate(sizes):
        if not size:
            continue
        unroll = UNROLL[kind]

        def body(i, carry, start=start, kind=kind, unroll=unroll):
            for u in range(unroll):
                job(start + i * unroll + u, [8.0 * c for c in range(CHUNKS[kind])])
            return carry

        lax.fori_loop(0, size // unroll, body, 0)
        start += size

    for kind, start, size, over in crowded:

        @pl.when(over)
        def _(kind=kind, start=start, size=size):
            def rest(j, carry):
                def one(c, inner):
                    job(start + j, [8.0 * c.astype(jnp.float32)])
                    return inner

                return lax.fori_loop(CHUNKS[kind], 16, one, carry)

            lax.fori_loop(0, size, rest, 0)


def bounds(st_ref, low, high):
    for t in range(TILES):
        value = st_ref[8 * t : 8 * t + 8, :]
        low[8 * t : 8 * t + 8, :] = jnp.broadcast_to(
            jnp.min(value, axis=1, keepdims=True), (8, G)
        )
        high[8 * t : 8 * t + 8, :] = jnp.broadcast_to(
            jnp.max(value, axis=1, keepdims=True), (8, G)
        )


def settle(acc):
    rows = []
    for t in range(TILES):
        for c in range(3):
            at = 24 * t + 8 * c
            rows.append(jnp.sum(acc[at : at + 8, :], axis=0, keepdims=True))
    return rows


def inner_kernel(sizes, count, tab_b, tab_c, st, part, ret, rel, total, fresh, *scr):
    *bridge, acc_a, acc_b, low, high, mark, keys, acc = scr
    acc_a[...] = jnp.zeros_like(acc_a)
    acc_b[...] = jnp.zeros_like(acc_b)
    acc[...] = jnp.zeros_like(acc)
    bounds(st, low, high)
    run_contacts(sizes, tab_c, st, st, ret, rel, ret, rel, low, high, mark, keys, acc)
    run_bridges(count, tab_b, st, st, part, ret, rel, bridge, acc_a, acc_b, fresh)
    rows = settle(acc)
    for t in range(TILES):
        at = 8 * t
        held = acc_a[at : at + 4, :] + acc_b[at : at + 4, :] + acc_b[at + 4 : at + 8, :]
        total[at : at + 4, :] = held
        for c in range(3):
            total[at + c : at + c + 1, :] = held[c : c + 1, :] + rows[3 * t + c]


def halo_kernel(
    sizes, n_out, n_in, tab_o, tab_i, tab_c, st, part, ret, rel, held, before,
    za, zb, ya, yb, xa, xb, forces, film, fresh, *scr
):
    *bridge, acc_a, acc_b, low, high, mark, keys, acc, halo, sems = scr
    copies = []
    for k, (pair, axis, at, rows) in enumerate(
        (((za, zb), "gz", Z_AT, Z_ROWS), ((ya, yb), "gy", Y_AT, Y_ROWS), ((xa, xb), "gx", X_AT, X_ROWS))
    ):
        odd = lax.axis_index(axis) % 2
        for w, src in enumerate(pair):
            side = (1 - odd) if w == 0 else odd
            copy = pltpu.make_async_copy(
                src, halo.at[pl.ds(at + side * rows, rows), :], sems.at[2 * k + w]
            )
            copy.start()
            copies.append(copy)
    keep = pltpu.make_async_copy(before, fresh, sems.at[6])
    keep.start()
    acc_a[...] = held[...]
    acc_b[...] = jnp.zeros_like(acc_b)
    acc[...] = jnp.zeros_like(acc)
    halo[ZERO_AT : ZERO_AT + 8, :] = jnp.zeros((8, G), jnp.float32)
    bounds(st, low, high)
    for copy in copies:
        copy.wait()
    keep.wait()
    run_contacts(sizes, tab_c, st, halo, ret, rel, halo, halo, low, high, mark, keys, acc)
    run_bridges(n_out, tab_o, st, halo, part, ret, rel, bridge, acc_a, None, fresh)
    run_bridges(n_in, tab_i, halo, st, halo, halo, halo, bridge, None, acc_b, None)
    rows = settle(acc)
    for t in range(TILES):
        at = 8 * t
        value = acc_a[at : at + 4, :] + acc_b[at : at + 4, :] + acc_b[at + 4 : at + 8, :]
        for c in range(3):
            forces[c, t : t + 1, :] = value[c : c + 1, :] + rows[3 * t + c]
        film[t : t + 1, :] = value[3:4, :] + st[at + 4 : at + 5, :]


def send_sides(axis):
    odd = lax.axis_index(axis) % 2
    return 1 - odd, odd


def own_slots(refs, at):
    return [ref[pl.ds(at, 9), :].astype(jnp.float32) for ref in refs]


def pack_z_kernel(pos, rad, film, part, ret, rel, st, out_a, out_b):
    for g in range(TILES // 8):
        members = [pos[c, 8 * g : 8 * g + 8, :] for c in range(3)]
        members += [rad[8 * g : 8 * g + 8, :], film[8 * g : 8 * g + 8, :]]
        for c, value in enumerate(members):
            st[pl.ds(64 * g + c, 8, stride=8), :] = value
        for c in range(5, 8):
            st[pl.ds(64 * g + c, 8, stride=8), :] = jnp.zeros((8, G), jnp.float32)
    for out, side in zip((out_a, out_b), send_sides("gz")):
        for xy in range(16):
            t = 2 * xy + side
            at = 32 * xy
            out[at : at + 5, :] = st[pl.ds(8 * t, 5), :]
            for k, ref in enumerate((part, ret, rel)):
                rows = ref[pl.ds(27 * t + 2 * side, 9, stride=3), :]
                out[at + 5 + 9 * k : at + 14 + 9 * k, :] = rows.astype(jnp.float32)


def load_sides(pair, axis, buf, rows, sems, first):
    odd = lax.axis_index(axis) % 2
    copies = []
    for w, src in enumerate(pair):
        side = (1 - odd) if w == 0 else odd
        copy = pltpu.make_async_copy(src, buf.at[pl.ds(side * rows, rows), :], sems.at[first + w])
        copy.start()
        copies.append(copy)
    return copies


def pack_y_kernel(st, part, ret, rel, za, zb, out_a, out_b, zbuf, sems):
    for copy in load_sides((za, zb), "gz", zbuf, Z_ROWS, sems, 0):
        copy.wait()
    for out, side in zip((out_a, out_b), send_sides("gy")):
        for x in range(4):
            for z in range(2):
                t = tile_number(x, 3 * side, z)
                at = 32 * (2 * x + z)
                out[at : at + 5, :] = st[pl.ds(8 * t, 5), :]
                for k, ref in enumerate((part, ret, rel)):
                    for i in range(3):
                        here = at + 5 + 9 * k + 3 * i
                        rows = ref[pl.ds(27 * t + 9 * i + 6 * side, 3), :]
                        out[here : here + 3, :] = rows.astype(jnp.float32)
        for sz in range(2):
            for x in range(4):
                at = 256 + 16 * (4 * sz + x)
                src = sz * Z_ROWS + (x * 4 + 3 * side) * 32
                out[at : at + 5, :] = zbuf[pl.ds(src, 5), :]
                for k in range(3):
                    out[at + 5 + 3 * k : at + 8 + 3 * k, :] = zbuf[
                        pl.ds(src + 5 + 9 * k + 2 * side, 3, stride=3), :
                    ]
                out[at + 14 : at + 16, :] = jnp.zeros((2, G), jnp.float32)


def pack_x_kernel(st, part, ret, rel, za, zb, ya, yb, out_a, out_b, zbuf, ybuf, sems):
    copies = load_sides((za, zb), "gz", zbuf, Z_ROWS, sems, 0)
    copies += load_sides((ya, yb), "gy", ybuf, Y_ROWS, sems, 2)
    for copy in copies:
        copy.wait()
    for out, side in zip((out_a, out_b), send_sides("gx")):
        for y in range(4):
            for z in range(2):
                t = tile_number(3 * side, y, z)
                at = 32 * (2 * y + z)
                out[at : at + 5, :] = st[pl.ds(8 * t, 5), :]
                for k, ref in enumerate((part, ret, rel)):
                    rows = ref[pl.ds(27 * t + 18 * side, 9), :]
                    out[at + 5 + 9 * k : at + 14 + 9 * k, :] = rows.astype(jnp.float32)
        for sy in range(2):
            for z in range(2):
                at = 256 + 16 * (2 * sy + z)
                src = sy * Y_ROWS + (2 * 3 * side + z) * 32
                out[at : at + 5, :] = ybuf[pl.ds(src, 5), :]
                for k in range(3):
                    out[at + 5 + 3 * k : at + 8 + 3 * k, :] = ybuf[
                        pl.ds(src + 5 + 9 * k + 6 * side, 3), :
                    ]
                out[at + 14 : at + 16, :] = jnp.zeros((2, G), jnp.float32)
        for sz in range(2):
            for y in range(4):
                at = 320 + 16 * (4 * sz + y)
                src = sz * Z_ROWS + (4 * 3 * side + y) * 32
                out[at : at + 5, :] = zbuf[pl.ds(src, 5), :]
                for k in range(3):
                    out[at + 5 + 3 * k : at + 8 + 3 * k, :] = zbuf[
                        pl.ds(src + 5 + 9 * k + 6 * side, 3), :
                    ]
                out[at + 14 : at + 16, :] = jnp.zeros((2, G), jnp.float32)
        for sy in range(2):
            for sz in range(2):
                at = 448 + 8 * (2 * sy + sz)
                src = sy * Y_ROWS + 256 + 16 * (4 * sz + 3 * side)
                out[at : at + 5, :] = ybuf[pl.ds(src, 5), :]
                for k in range(3):
                    out[at + 5 + k : at + 6 + k, :] = ybuf[
                        pl.ds(src + 5 + 3 * k + 2 * side, 1), :
                    ]


VM = pl.BlockSpec(memory_space=pltpu.VMEM)
SM = pl.BlockSpec(memory_space=pltpu.SMEM)
AN = pl.BlockSpec(memory_space=pl.ANY)
PARAMS = pltpu.CompilerParams(vmem_limit_bytes=48 * 1024 * 1024)


def rows_of(n):
    return jax.ShapeDtypeStruct((n, G), jnp.float32)


def swap(pair, axis):
    count = lax.axis_size(axis)
    first, second = pair
    near = [(i, i ^ 1) for i in range(count) if i ^ 1 < count]
    far = [(i, ((i + 1) ^ 1) - 1) for i in range(1, count) if ((i + 1) ^ 1) - 1 < count]
    return lax.ppermute(first, axis, near), lax.ppermute(second, axis, far)


def bridge_scratch():
    return [
        pltpu.VMEM((8 * BATCH, G), jnp.float32),
        pltpu.VMEM((8 * BATCH, G), jnp.float32),
        pltpu.VMEM((BATCH, G), jnp.float32),
        pltpu.VMEM((BATCH, G), jnp.float32),
        pltpu.VMEM((8 * BATCH, G), jnp.float32),
        pltpu.VMEM((8 * BATCH, G), jnp.float32),
    ]


def work_scratch(jobs):
    return bridge_scratch() + [
        pltpu.VMEM((8 * TILES, G), jnp.float32),
        pltpu.VMEM((8 * TILES, G), jnp.float32),
        pltpu.VMEM((8 * TILES, G), jnp.float32),
        pltpu.VMEM((8 * TILES, G), jnp.float32),
        pltpu.VMEM((jobs, G), jnp.float32),
        pltpu.VMEM((jobs, G), jnp.float32),
        pltpu.VMEM((24 * TILES, G), jnp.float32),
    ]


def shards(positions, grain_radii, film_liquid, pair_live, partner, rupture, volume):
    pos = positions.reshape(3, TILES, G)
    rad = grain_radii.reshape(TILES, G)
    film = film_liquid.reshape(TILES, G)
    part = partner.reshape(SLOTS, G)
    vol = volume.reshape(SLOTS, G)
    live = pair_live.reshape(SLOTS, 1) > 0
    broken = rupture.reshape(SLOTS, G) > 0
    ret = jnp.where(live & ~broken, vol, 0.0)
    rel = jnp.where(live & broken, vol, 0.0)

    st, za, zb = pl.pallas_call(
        pack_z_kernel,
        out_shape=(rows_of(8 * TILES), rows_of(Z_ROWS), rows_of(Z_ROWS)),
        in_specs=[VM] * 6,
        out_specs=(VM,) * 3,
        compiler_params=PARAMS,
        name="pack_z",
    )(pos, rad, film, part, ret, rel)
    za, zb = swap((za, zb), "gz")
    ya, yb = pl.pallas_call(
        pack_y_kernel,
        out_shape=(rows_of(Y_ROWS),) * 2,
        in_specs=[VM] * 4 + [AN] * 2,
        out_specs=(VM,) * 2,
        scratch_shapes=[pltpu.VMEM((2 * Z_ROWS, G), jnp.float32), pltpu.SemaphoreType.DMA((2,))],
        compiler_params=PARAMS,
        name="pack_y",
    )(st, part, ret, rel, za, zb)
    ya, yb = swap((ya, yb), "gy")
    xa, xb = pl.pallas_call(
        pack_x_kernel,
        out_shape=(rows_of(X_ROWS),) * 2,
        in_specs=[VM] * 4 + [AN] * 4,
        out_specs=(VM,) * 2,
        scratch_shapes=[
            pltpu.VMEM((2 * Z_ROWS, G), jnp.float32),
            pltpu.VMEM((2 * Y_ROWS, G), jnp.float32),
            pltpu.SemaphoreType.DMA((4,)),
        ],
        compiler_params=PARAMS,
        name="pack_x",
    )(st, part, ret, rel, za, zb, ya, yb)
    xa, xb = swap((xa, xb), "gx")

    inner, outward, inward = bridge_tables()
    near = contact_tables(False)
    zero = SLOTS
    near = [pad(rows, UNROLL[k] if k else 16, (0, 0, zero, zero, zero)) for k, rows in enumerate(near)]
    inner = pad(inner, BATCH, (0, 0, zero, zero, zero))
    sizes = tuple(len(rows) for rows in near)
    extra = jnp.zeros((8, G), jnp.float32)
    part_pad = jnp.concatenate([part, jnp.zeros((8, G), jnp.int32)], axis=0)
    ret_pad = jnp.concatenate([ret, extra], axis=0)
    rel_pad = jnp.concatenate([rel, extra], axis=0)
    tab_c = flat(sum(near, []))
    tab_b = flat(inner)
    held, fresh = pl.pallas_call(
        functools.partial(inner_kernel, sizes, len(inner)),
        out_shape=(rows_of(8 * TILES), rows_of(SLOTS + 8)),
        in_specs=[SM] * 2 + [VM] * 4,
        out_specs=(VM,) * 2,
        scratch_shapes=work_scratch(sum(sizes)),
        compiler_params=PARAMS,
        name="inner",
    )(tab_b, tab_c, st, part_pad, ret_pad, rel_pad)

    far = contact_tables(True)
    far = [pad(rows, UNROLL[k] if k else 16, (0, 0, zero, ZERO_AT, ZERO_AT)) for k, rows in enumerate(far)]
    sizes = tuple(len(rows) for rows in far)
    outward = pad(outward, BATCH, (0, 0, zero, zero, zero))
    inward = pad(inward, BATCH, (0, 0, ZERO_AT, ZERO_AT, ZERO_AT))
    forces, film_next, fresh = pl.pallas_call(
        functools.partial(halo_kernel, sizes, len(outward), len(inward)),
        out_shape=(
            jax.ShapeDtypeStruct((3, TILES, G), jnp.float32),
            rows_of(TILES),
            rows_of(SLOTS + 8),
        ),
        in_specs=[SM] * 3 + [VM] * 5 + [AN] * 7,
        out_specs=(VM,) * 3,
        scratch_shapes=work_scratch(sum(sizes))
        + [pltpu.VMEM((HALO_ROWS, G), jnp.float32), pltpu.SemaphoreType.DMA((7,))],
        compiler_params=PARAMS,
        name="halo",
    )(
        flat(outward), flat(inward), flat(sum(far, [])),
        st, part_pad, ret_pad, rel_pad, held, fresh, za, zb, ya, yb, xa, xb,
    )
    return (
        forces.reshape(positions.shape),
        film_next.reshape(film_liquid.shape),
        fresh[:SLOTS].reshape(volume.shape),
    )


def solution(mesh):
    return jax.shard_map(
        shards,
        mesh=mesh,
        in_specs=(
            P(None, "gx", "gy", "gz", None),
            P("gx", "gy", "gz", None),
            P("gx", "gy", "gz", None),
            P("gx", "gy", "gz", None),
            P("gx", "gy", "gz", None, None),
            P("gx", "gy", "gz", None, None),
            P("gx", "gy", "gz", None, None),
        ),
        out_specs=(
            P(None, "gx", "gy", "gz", None),
            P("gx", "gy", "gz", None),
            P("gx", "gy", "gz", None, None),
        ),
        check_vma=False,
    )
```

time: 335 us -> 89.3 us (0.27)
  the two profiles are of different devices: /device:TPU:169 before, /device:TPU:108 now
where the time goes in v1:
time: 89.3 us; the launch traced here: 87.7 us
  Pallas kernels  59.3 us (66%)
  waiting for transfers between devices  12.6 us (14%)
  starting transfers between devices  10.2 us (11%)
  local copies, waits for them, and re-layouts  2.37 us (3%)
  other arithmetic  2.27 us (3%)
    pallas_call x1, Pallas kernels, shards(): pl.pallas_call(functools.partial(halo_kernel, sizes, len(outward), len(in...  31.9 us
    pallas_call x1, Pallas kernels, shards(): pl.pallas_call(functools.partial(inner_kernel, sizes, len(inner)), out_sh...  26.5 us
    ppermute x6, waiting for transfers between devices, swap(): return (lax.ppermute(first, axis, near), lax.ppermute(second, axis, far))  12.6 us
    ppermute x6, starting transfers between devices, swap(): return (lax.ppermute(first, axis, near), lax.ppermute(second, axis, far))  10.2 us
  transfers between devices with their start and end apart: 6, of which 3 were waited for; matrix products, arithmetic and copies ran while one was open for 0% of the time, Pallas kernels for 30%

profile of v1, /device:TPU:108, one launch (start us, length us, event | category | flops | bytes accessed | tf_op | source)
XLA Modules:
  0.0 87.7 jit_solution(10937096414295755672)
XLA Ops:
  0.6 0.7 compare_reduce_fusion
  1.3 1.4 %bitcast_select_fusion = (f32[864,128]{1,0:T(8,128)S(1)}, pred[1,1,1,864,128]{4,3,2,1,0:T(8,128)(4,1)S(1)}) fusion(f32[1,1,1,864,128]{4,3,2,1,0:T(8,128)} %param.18, pred[864]{0:T(1024)(128)(4,1)S(1)} %compare_reduce_fusion, s32[1,1,1,864,128]{4,3,2,1,0:T(8,128)} %param.17), kind=kLoop, calls=%fused_computation | loop fusion | flops 331776 | bytes 1438560 | tf_op jit(solution)/shard_map/jit(_where)/select_n | solution.py:552
  2.7 0.0 copy-done.9
  2.7 0.0 copy-start
  2.8 0.0 copy-start.1
  2.8 0.0 copy-start.2
  2.8 0.0 copy-start.3
  2.8 0.2 bitcast_select_fusion.1.ret
  3.0 0.8 copy-done
  3.8 0.0 copy-done.2
  3.8 0.1 pack_z.1
  3.9 1.3 %collective-permute-start = (f32[512,128]{1,0:T(8,128)S(1)}, f32[512,128]{1,0:T(8,128)S(1)}, u32[]{:S(2)}, u32[]{:S(2)}) collective-permute-start(f32[512,128]{1,0:T(8,128)S(1)} %get-tuple-element.18), channel_id=1, source_target_pairs={{0,1},{1,0},{2,3},{3,2},{4,5},{5,4},{6,7},{7,6},{8,9},{9,8},{10,11... | collective-permute-start | bytes 786440 | tf_op jit(solution)/shard_map/ppermute | solution.py:517
  5.2 1.9 %collective-permute-start.1 = (f32[512,128]{1,0:T(8,128)S(1)}, f32[512,128]{1,0:T(8,128)S(1)}, u32[]{:S(2)}, u32[]{:S(2)}) collective-permute-start(f32[512,128]{1,0:T(8,128)S(1)} %get-tuple-element.19), channel_id=1, source_target_pairs={{1,2},{2,1},{5,6},{6,5},{9,10},{10,9},{13,14},{14,13},{17,18},{18,... | collective-permute-start | bytes 786440 | tf_op jit(solution)/shard_map/ppermute | solution.py:517
  7.1 4.9 %collective-permute-done.za = f32[512,128]{1,0:T(8,128)S(1)} collective-permute-done((f32[512,128]{1,0:T(8,128)S(1)}, f32[512,128]{1,0:T(8,128)S(1)}, u32[]{:S(2)}, u32[]{:S(2)}) %collective-permute-start) | collective-permute-done | bytes 262176 | tf_op jit(solution)/shard_map/ppermute | solution.py:517
  12.0 2.8 %collective-permute-done.1.zb = f32[512,128]{1,0:T(8,128)S(1)} collective-permute-done((f32[512,128]{1,0:T(8,128)S(1)}, f32[512,128]{1,0:T(8,128)S(1)}, u32[]{:S(2)}, u32[]{:S(2)}) %collective-permute-start.1) | collective-permute-done | bytes 262176 | tf_op jit(solution)/shard_map/ppermute | solution.py:517
  14.8 0.2 pack_y.1
  15.0 0.1 collective-permute-start.2
  15.1 2.1 %collective-permute-start.3 = (f32[384,128]{1,0:T(8,128)S(1)}, f32[384,128]{1,0:T(8,128)S(1)}, u32[]{:S(2)}, u32[]{:S(2)}) collective-permute-start(f32[384,128]{1,0:T(8,128)S(1)} %get-tuple-element.21), channel_id=1, source_target_pairs={{4,8},{8,4},{12,16},{16,12},{20,24},{24,20},{28,32},{32,28},{36,40... | collective-permute-start | bytes 589832 | tf_op jit(solution)/shard_map/ppermute | solution.py:517
  17.2 0.0 collective-permute-done.2.ya
  17.2 4.9 %collective-permute-done.3.yb = f32[384,128]{1,0:T(8,128)S(1)} collective-permute-done((f32[384,128]{1,0:T(8,128)S(1)}, f32[384,128]{1,0:T(8,128)S(1)}, u32[]{:S(2)}, u32[]{:S(2)}) %collective-permute-start.3) | collective-permute-done | bytes 196640 | tf_op jit(solution)/shard_map/ppermute | solution.py:517
  22.1 0.7 pack_x.1
  22.8 0.5 collective-permute-start.4
  23.3 4.3 %collective-permute-start.5 = (f32[480,128]{1,0:T(8,128)S(1)}, f32[480,128]{1,0:T(8,128)S(1)}, u32[]{:S(2)}, u32[]{:S(2)}) collective-permute-start(f32[480,128]{1,0:T(8,128)S(1)} %get-tuple-element.23), channel_id=1, source_target_pairs={{64,128},{128,64},{65,129},{129,65},{66,130},{130,66},{67,131},{13... | collective-permute-start | bytes 737288 | tf_op jit(solution)/shard_map/ppermute | solution.py:517
  27.7 0.0 copy-start.7
  27.7 0.0 copy-start.8
  27.7 0.6 copy-done.7
  28.4 0.0 copy-done.8
  28.4 26.5 %inner.1 = (f32[256,128]{1,0:T(8,128)S(1)}, f32[872,128]{1,0:T(8,128)S(1)}) custom-call(s32[2080]{0:T(1024)S(1)} %copy-done.7, s32[2000]{0:T(1024)S(1)} %copy-done.8, f32[256,128]{1,0:T(8,128)S(1)} %get-tuple-element.15.st, s32[872,128]{1,0:T(8,128)S(1)} %concatenate.9.part, f32[872,128]{1,0:T(8,128)S(1)} %concatenate.10.ret, f32[872,128]{1,0:T(8,128)S(1)} %concatenate.11.rel), custom_call_target="tpu_custom_call" | custom-call | tf_op jit(solution)/shard_map/inner/pallas_call | solution.py:600
  54.9 0.0 collective-permute-done.4.xa
  54.9 0.0 collective-permute-done.5.xb
  55.0 31.9 %halo.1 = (f32[3,32,128]{2,1,0:T(8,128)}, f32[32,128]{1,0:T(8,128)}, f32[872,128]{1,0:T(8,128)S(1)}) custom-call(s32[2400]{0:T(1024)S(1)} %copy-done.6, s32[2400]{0:T(1024)S(1)} %copy-done.5, s32[2320]{0:T(1024)S(1)} %copy-done.4, f32[256,128]{1,0:T(8,128)S(1)} %get-tuple-element.15.st, s32[872,128]{1,0:T(8,128)S(1)} %concatenate.9.part, ...), custom_call_target="tpu_custom_call" | custom-call | tf_op jit(solution)/shard_map/halo/pallas_call | solution.py:615
  86.9 0.8 slice_bitcast_fusion
  (12 shorter events, 0.1 us)
Async XLA Ops:
  1.3 1.4 %copy-start.9 = (f32[1,1,1,864,128]{4,3,2,1,0:T(8,128)S(1)}, f32[1,1,1,864,128]{4,3,2,1,0:T(8,128)}, u32[]{:S(2)}) copy-start(f32[1,1,1,864,128]{4,3,2,1,0:T(8,128)} %param.18) | copy-start | bytes 1327108
  2.7 1.0 %copy-start = (s32[1,1,1,864,128]{4,3,2,1,0:T(8,128)S(1)}, s32[1,1,1,864,128]{4,3,2,1,0:T(8,128)}, u32[]{:S(2)}) copy-start(s32[1,1,1,864,128]{4,3,2,1,0:T(8,128)} %param.16) | copy-start | bytes 1327108
  2.8 1.0 %copy-start.1 = (f32[3,4,4,2,128]{4,3,2,1,0:T(2,128)S(1)}, f32[3,4,4,2,128]{4,3,2,1,0:T(2,128)}, u32[]{:S(2)}) copy-start(f32[3,4,4,2,128]{4,3,2,1,0:T(2,128)} %param.12) | copy-start | bytes 147460
  2.8 1.0 %copy-start.2 = (f32[4,4,2,128]{3,2,1,0:T(2,128)S(1)}, f32[4,4,2,128]{3,2,1,0:T(2,128)}, u32[]{:S(2)}) copy-start(f32[4,4,2,128]{3,2,1,0:T(2,128)} %param.13) | copy-start | bytes 49156
  2.8 1.0 %copy-start.3 = (f32[4,4,2,128]{3,2,1,0:T(2,128)S(1)}, f32[4,4,2,128]{3,2,1,0:T(2,128)}, u32[]{:S(2)}) copy-start(f32[4,4,2,128]{3,2,1,0:T(2,128)} %param.14) | copy-start | bytes 49156
  3.9 8.1 %collective-permute-start = (f32[512,128]{1,0:T(8,128)S(1)}, f32[512,128]{1,0:T(8,128)S(1)}, u32[]{:S(2)}, u32[]{:S(2)}) collective-permute-start(f32[512,128]{1,0:T(8,128)S(1)} %get-tuple-element.18), channel_id=1, source_target_pairs={{0,1},{1,0},{2,3},{3,2},{4,5},{5,4},{6,7},{7,6},{8,9},{9,8},{10,11... | collective-permute-start | bytes 786440 | tf_op jit(solution)/shard_map/ppermute | solution.py:517
  5.2 9.6 %collective-permute-start.1 = (f32[512,128]{1,0:T(8,128)S(1)}, f32[512,128]{1,0:T(8,128)S(1)}, u32[]{:S(2)}, u32[]{:S(2)}) collective-permute-start(f32[512,128]{1,0:T(8,128)S(1)} %get-tuple-element.19), channel_id=1, source_target_pairs={{1,2},{2,1},{5,6},{6,5},{9,10},{10,9},{13,14},{14,13},{17,18},{18,... | collective-permute-start | bytes 786440 | tf_op jit(solution)/shard_map/ppermute | solution.py:517
  15.0 2.2 %collective-permute-start.2 = (f32[384,128]{1,0:T(8,128)S(1)}, f32[384,128]{1,0:T(8,128)S(1)}, u32[]{:S(2)}, u32[]{:S(2)}) collective-permute-start(f32[384,128]{1,0:T(8,128)S(1)} %get-tuple-element.20), channel_id=1, source_target_pairs={{0,4},{4,0},{8,12},{12,8},{16,20},{20,16},{24,28},{28,24},{32,36},... | collective-permute-start | bytes 589832 | tf_op jit(solution)/shard_map/ppermute | solution.py:517
  15.1 7.0 %collective-permute-start.3 = (f32[384,128]{1,0:T(8,128)S(1)}, f32[384,128]{1,0:T(8,128)S(1)}, u32[]{:S(2)}, u32[]{:S(2)}) collective-permute-start(f32[384,128]{1,0:T(8,128)S(1)} %get-tuple-element.21), channel_id=1, source_target_pairs={{4,8},{8,4},{12,16},{16,12},{20,24},{24,20},{28,32},{32,28},{36,40... | collective-permute-start | bytes 589832 | tf_op jit(solution)/shard_map/ppermute | solution.py:517
  22.8 32.2 %collective-permute-start.4 = (f32[480,128]{1,0:T(8,128)S(1)}, f32[480,128]{1,0:T(8,128)S(1)}, u32[]{:S(2)}, u32[]{:S(2)}) collective-permute-start(f32[480,128]{1,0:T(8,128)S(1)} %get-tuple-element.22), channel_id=1, source_target_pairs={{0,64},{64,0},{128,192},{192,128},{1,65},{65,1},{129,193},{193,129... | collective-permute-start | bytes 737288 | tf_op jit(solution)/shard_map/ppermute | solution.py:517
  23.3 31.6 %collective-permute-start.5 = (f32[480,128]{1,0:T(8,128)S(1)}, f32[480,128]{1,0:T(8,128)S(1)}, u32[]{:S(2)}, u32[]{:S(2)}) collective-permute-start(f32[480,128]{1,0:T(8,128)S(1)} %get-tuple-element.23), channel_id=1, source_target_pairs={{64,128},{128,64},{65,129},{129,65},{66,130},{130,66},{67,131},{13... | collective-permute-start | bytes 737288 | tf_op jit(solution)/shard_map/ppermute | solution.py:517
  27.7 0.7 copy-start.7
  27.7 0.7 copy-start.8
  28.4 26.5 %copy-start.4 = (s32[2320]{0:T(1024)S(1)}, s32[2320]{0:T(1024)}, u32[]{:S(2)}) copy-start(s32[2320]{0:T(1024)} %constant.21.clone.tab_c) | copy-start | bytes 27844
  28.4 26.5 %copy-start.5 = (s32[2400]{0:T(1024)S(1)}, s32[2400]{0:T(1024)}, u32[]{:S(2)}) copy-start(s32[2400]{0:T(1024)} %constant.20.clone.tab_i) | copy-start | bytes 28804
  28.4 26.5 %copy-start.6 = (s32[2400]{0:T(1024)S(1)}, s32[2400]{0:T(1024)}, u32[]{:S(2)}) copy-start(s32[2400]{0:T(1024)} %constant.6.clone.tab_o) | copy-start | bytes 28804

commit v2 on v1

--- a/solution.py
+++ b/solution.py
@@ -82,7 +82,7 @@
 
 
 def bridge_tables():
-    inner, outward, inward = [], [], []
+    inner, outward, inward = [], [], [[], [], [], []]
     for t, e, b in pairs():
         own = 8 * tile_number(*t)
         s = 27 * tile_number(*t) + code(e)
@@ -91,8 +91,8 @@
         else:
             back = tuple(-v for v in e)
             outward.append((own, halo_block(*b)[0], s, s, s))
-            inward.append((halo_block(*b)[0], own) + halo_slot(*b, back))
-    return inner, outward, inward
+            inward[contact_class(e)].append((halo_block(*b)[0], own) + halo_slot(*b, back))
+    return inner, outward, sum(inward, [])
 
 
 def contact_class(e):
@@ -105,7 +105,7 @@
 
 
 CHUNKS = (1, 2, 4, 16)
-UNROLL = (16, 8, 4, 2)
+UNROLL = (80, 16, 16, 4)
 
 
 def contact_tables(halo):
@@ -137,13 +137,27 @@
     return ref[pl.ds(pl.multiple_of(at, 8), 8), :]
 
 
-def run_bridges(count, tab, a_ref, b_ref, p_ref, q_ref, l_ref, scr, acc_a, acc_b, next_ref):
+def compact(count, listed, jobs):
+    def body(i, n):
+        for u in range(16):
+            j = i * 16 + u
+            jobs[n] = j
+            n = n + listed(j)
+        return n
+
+    n = lax.fori_loop(0, count // 16, body, 0)
+    for u in range(BATCH):
+        jobs[n + u] = count
+    return (n + BATCH - 1) // BATCH
+
+
+def run_bridges(batches, jobs, tab, a_ref, b_ref, p_ref, q_ref, l_ref, scr, acc_a, acc_b, next_ref):
     m_ref, a_scr, q_scr, l_scr, f_ref, g_ref = scr
 
     def body(i, carry):
         at = []
         for j in range(BATCH):
-            o = (i * BATCH + j) * 5
+            o = jobs[i * BATCH + j] * 5
             at.append([tab[o + k] for k in range(5)])
         partner = []
         for j in range(BATCH):
@@ -208,7 +222,7 @@
                 acc_b[here, :] = acc_b[here, :] + landed
         return carry
 
-    lax.fori_loop(0, count // BATCH, body, 0)
+    lax.fori_loop(0, batches, body, 0)
 
 
 def chunk_force(key, base, other, target):
@@ -229,15 +243,19 @@
     return [push * delta[c] for c in range(3)]
 
 
-def run_contacts(sizes, tab, t_ref, n_ref, q_ref, l_ref, nq_ref, nl_ref, low, high, mark, keys, acc):
+def run_contacts(sizes, tab, t_ref, n_ref, q_ref, l_ref, nq_ref, nl_ref, low, high, mark, keys, seen, acc):
     total = sum(sizes)
+    step = max(k for k in range(1, 81) if total % k == 0)
     wide = lax.broadcasted_iota(jnp.int32, (8, G), 0)
 
     def near(i, carry):
-        for u in range(16):
-            j = i * 16 + u
+        for u in range(step):
+            j = i * step + u
             t, n, s, nq, nl = [tab[j * 5 + k] for k in range(5)]
-            live = row(q_ref, s) + row(l_ref, s) + row(nq_ref, nq) + row(nl_ref, nl) > 0.0
+            theirs = row(nq_ref, nq) + row(nl_ref, nl)
+            if seen is not None:
+                seen[pl.ds(j, 1), :] = theirs
+            live = row(q_ref, s) + row(l_ref, s) + theirs > 0.0
             value = block(n_ref, n)
             top = block(high, t)
             gap = jnp.maximum(jnp.maximum(block(low, t) - value, value - top), 0.0)
@@ -249,7 +267,7 @@
             )
         return carry
 
-    lax.fori_loop(0, total // 16, near, 0)
+    lax.fori_loop(0, total // step, near, 0)
     lane = lax.broadcasted_iota(jnp.int32, (G, G), 1)
     sub = lax.broadcasted_iota(jnp.int32, (G, G), 0)
     upper = (sub <= lane).astype(jnp.bfloat16)
@@ -334,28 +352,39 @@
     return rows
 
 
-def inner_kernel(sizes, count, tab_b, tab_c, st, part, ret, rel, total, fresh, *scr):
-    *bridge, acc_a, acc_b, low, high, mark, keys, acc = scr
-    acc_a[...] = jnp.zeros_like(acc_a)
-    acc_b[...] = jnp.zeros_like(acc_b)
+def contact_kernel(sizes, tab_c, st, ret, rel, before, after, total, *scr):
+    low, high, mark, keys, acc = scr
     acc[...] = jnp.zeros_like(acc)
     bounds(st, low, high)
-    run_contacts(sizes, tab_c, st, st, ret, rel, ret, rel, low, high, mark, keys, acc)
-    run_bridges(count, tab_b, st, st, part, ret, rel, bridge, acc_a, acc_b, fresh)
+    run_contacts(sizes, tab_c, st, st, ret, rel, ret, rel, low, high, mark, keys, None, acc)
     rows = settle(acc)
     for t in range(TILES):
         at = 8 * t
-        held = acc_a[at : at + 4, :] + acc_b[at : at + 4, :] + acc_b[at + 4 : at + 8, :]
-        total[at : at + 4, :] = held
+        total[at : at + 8, :] = jnp.zeros((8, G), jnp.float32) if before is None else before[at : at + 8, :]
         for c in range(3):
-            total[at + c : at + c + 1, :] = held[c : c + 1, :] + rows[3 * t + c]
+            total[at + c : at + c + 1, :] = total[at + c : at + c + 1, :] + rows[3 * t + c]
+
+
+def bridge_kernel(count, tab_b, live, st, part, ret, rel, before, after, total, fresh, *scr):
+    *bridge, acc_a, acc_b, jobs = scr
+    acc_a[...] = before[...]
+    acc_b[...] = jnp.zeros_like(acc_b)
+    fresh[...] = jnp.zeros_like(fresh)
+    batches = compact(count, lambda j: live[tab_b[j * 5 + 2]], jobs)
+    run_bridges(batches, jobs, tab_b, st, st, part, ret, rel, bridge, acc_a, acc_b, fresh)
+    for t in range(TILES):
+        at = 8 * t
+        total[at : at + 4, :] = (
+            acc_a[at : at + 4, :] + acc_b[at : at + 4, :] + acc_b[at + 4 : at + 8, :]
+        )
+        total[at + 4 : at + 8, :] = jnp.zeros((4, G), jnp.float32)
 
 
 def halo_kernel(
-    sizes, n_out, n_in, tab_o, tab_i, tab_c, st, part, ret, rel, held, before,
+    sizes, n_out, n_in, tab_o, tab_i, tab_c, live, st, part, ret, rel, held, before,
     za, zb, ya, yb, xa, xb, forces, film, fresh, *scr
 ):
-    *bridge, acc_a, acc_b, low, high, mark, keys, acc, halo, sems = scr
+    *bridge, acc_a, acc_b, low, high, mark, keys, seen, acc, halo, flag, jobs_o, jobs_i, flags, sems = scr
     copies = []
     for k, (pair, axis, at, rows) in enumerate(
         (((za, zb), "gz", Z_AT, Z_ROWS), ((ya, yb), "gy", Y_AT, Y_ROWS), ((xa, xb), "gx", X_AT, X_ROWS))
@@ -375,12 +404,28 @@
     acc[...] = jnp.zeros_like(acc)
     halo[ZERO_AT : ZERO_AT + 8, :] = jnp.zeros((8, G), jnp.float32)
     bounds(st, low, high)
+    out_batches = compact(n_out, lambda j: live[tab_o[j * 5 + 2]], jobs_o)
     for copy in copies:
         copy.wait()
     keep.wait()
-    run_contacts(sizes, tab_c, st, halo, ret, rel, halo, halo, low, high, mark, keys, acc)
-    run_bridges(n_out, tab_o, st, halo, part, ret, rel, bridge, acc_a, None, fresh)
-    run_bridges(n_in, tab_i, halo, st, halo, halo, halo, bridge, None, acc_b, None)
+    run_contacts(sizes, tab_c, st, halo, ret, rel, halo, halo, low, high, mark, keys, seen, acc)
+    first = (
+        lax.broadcasted_iota(jnp.int32, (8, G), 0) + lax.broadcasted_iota(jnp.int32, (8, G), 1)
+    ) == 0
+    listed = lax.dot_general(
+        first.astype(jnp.bfloat16),
+        (seen[...] > 0.0).astype(jnp.bfloat16),
+        (((1,), (1,)), ((), ())),
+        preferred_element_type=jnp.float32,
+    )
+    for k in range(4):
+        flag[k : k + 1, :] = listed[0:1, k * G : k * G + G].astype(jnp.int32)
+    down = pltpu.make_async_copy(flag, flags, sems.at[7])
+    down.start()
+    run_bridges(out_batches, jobs_o, tab_o, st, halo, part, ret, rel, bridge, acc_a, None, fresh)
+    down.wait()
+    in_batches = compact(n_in, lambda j: flags[j // G, j % G], jobs_i)
+    run_bridges(in_batches, jobs_i, tab_i, halo, st, halo, halo, halo, bridge, None, acc_b, None)
     rows = settle(acc)
     for t in range(TILES):
         at = 8 * t
@@ -428,7 +473,7 @@
     return copies
 
 
-def pack_y_kernel(st, part, ret, rel, za, zb, out_a, out_b, zbuf, sems):
+def pack_y_kernel(st, part, ret, rel, za, zb, after, out_a, out_b, zbuf, sems):
     for copy in load_sides((za, zb), "gz", zbuf, Z_ROWS, sems, 0):
         copy.wait()
     for out, side in zip((out_a, out_b), send_sides("gy")):
@@ -454,7 +499,7 @@
                 out[at + 14 : at + 16, :] = jnp.zeros((2, G), jnp.float32)
 
 
-def pack_x_kernel(st, part, ret, rel, za, zb, ya, yb, out_a, out_b, zbuf, ybuf, sems):
+def pack_x_kernel(st, part, ret, rel, za, zb, ya, yb, after, out_a, out_b, zbuf, ybuf, sems):
     copies = load_sides((za, zb), "gz", zbuf, Z_ROWS, sems, 0)
     copies += load_sides((ya, yb), "gy", ybuf, Y_ROWS, sems, 2)
     for copy in copies:
@@ -528,16 +573,15 @@
     ]
 
 
-def work_scratch(jobs):
-    return bridge_scratch() + [
-        pltpu.VMEM((8 * TILES, G), jnp.float32),
-        pltpu.VMEM((8 * TILES, G), jnp.float32),
-        pltpu.VMEM((8 * TILES, G), jnp.float32),
-        pltpu.VMEM((8 * TILES, G), jnp.float32),
-        pltpu.VMEM((jobs, G), jnp.float32),
-        pltpu.VMEM((jobs, G), jnp.float32),
-        pltpu.VMEM((24 * TILES, G), jnp.float32),
-    ]
+def tiles_scratch(count):
+    return [pltpu.VMEM((8 * TILES, G), jnp.float32)] * count
+
+
+def contact_scratch(jobs, halo):
+    out = tiles_scratch(2) + [pltpu.VMEM((jobs, G), jnp.float32)] * 2
+    if halo:
+        out = out + [pltpu.VMEM((512, G), jnp.float32)]
+    return out + [pltpu.VMEM((24 * TILES, G), jnp.float32)]
 
 
 def shards(positions, grain_radii, film_liquid, pair_live, partner, rupture, volume):
@@ -559,21 +603,64 @@
         compiler_params=PARAMS,
         name="pack_z",
     )(pos, rad, film, part, ret, rel)
+    zero = SLOTS
+    extra = jnp.zeros((8, G), jnp.float32)
+    part_pad = jnp.concatenate([part, jnp.zeros((8, G), jnp.int32)], axis=0)
+    ret_pad = jnp.concatenate([ret, extra], axis=0)
+    rel_pad = jnp.concatenate([rel, extra], axis=0)
+    flags = pair_live.reshape(SLOTS)
+
+    def contacts(kinds, before, after, name):
+        near = contact_tables(False)
+        near = [
+            pad(near[k], UNROLL[k], (0, 0, zero, zero, zero)) if k in kinds else [] for k in range(4)
+        ]
+        sizes = tuple(len(rows) for rows in near)
+        body = contact_kernel
+        if before is None:
+            body = lambda sizes, tab, st, ret, rel, after, *rest: contact_kernel(
+                sizes, tab, st, ret, rel, None, after, *rest
+            )
+        given = [] if before is None else [before]
+        return pl.pallas_call(
+            functools.partial(body, sizes),
+            out_shape=rows_of(8 * TILES),
+            in_specs=[SM] + [VM] * (3 + len(given)) + [AN],
+            out_specs=VM,
+            scratch_shapes=contact_scratch(sum(sizes), False),
+            compiler_params=PARAMS,
+            name=name,
+        )(flat(sum(near, [])), st, ret_pad, rel_pad, *given, after)
+
+    inner, outward, inward = bridge_tables()
+    dummy = (0, 0, zero, zero, zero)
     za, zb = swap((za, zb), "gz")
+    held = contacts((3, 1), None, st, "contact_own")
     ya, yb = pl.pallas_call(
         pack_y_kernel,
         out_shape=(rows_of(Y_ROWS),) * 2,
-        in_specs=[VM] * 4 + [AN] * 2,
+        in_specs=[VM] * 4 + [AN] * 3,
         out_specs=(VM,) * 2,
         scratch_shapes=[pltpu.VMEM((2 * Z_ROWS, G), jnp.float32), pltpu.SemaphoreType.DMA((2,))],
         compiler_params=PARAMS,
         name="pack_y",
-    )(st, part, ret, rel, za, zb)
-    ya, yb = swap((ya, yb), "gy")
+    )(st, part, ret, rel, za, zb, held)
+    ya, yb, order_y = *swap((ya, yb), "gy"), ya
+    held, fresh = pl.pallas_call(
+        functools.partial(bridge_kernel, len(inner)),
+        out_shape=(rows_of(8 * TILES), rows_of(SLOTS + 8)),
+        in_specs=[SM] * 2 + [VM] * 5 + [AN],
+        out_specs=(VM,) * 2,
+        scratch_shapes=bridge_scratch()
+        + tiles_scratch(2)
+        + [pltpu.SMEM((len(inner) + BATCH,), jnp.int32)],
+        compiler_params=PARAMS,
+        name="bridge_own",
+    )(flat(inner + [dummy]), flags, st, part_pad, ret_pad, rel_pad, held, order_y)
     xa, xb = pl.pallas_call(
         pack_x_kernel,
         out_shape=(rows_of(X_ROWS),) * 2,
-        in_specs=[VM] * 4 + [AN] * 4,
+        in_specs=[VM] * 4 + [AN] * 5,
         out_specs=(VM,) * 2,
         scratch_shapes=[
             pltpu.VMEM((2 * Z_ROWS, G), jnp.float32),
@@ -582,36 +669,13 @@
         ],
         compiler_params=PARAMS,
         name="pack_x",
-    )(st, part, ret, rel, za, zb, ya, yb)
-    xa, xb = swap((xa, xb), "gx")
-
-    inner, outward, inward = bridge_tables()
-    near = contact_tables(False)
-    zero = SLOTS
-    near = [pad(rows, UNROLL[k] if k else 16, (0, 0, zero, zero, zero)) for k, rows in enumerate(near)]
-    inner = pad(inner, BATCH, (0, 0, zero, zero, zero))
-    sizes = tuple(len(rows) for rows in near)
-    extra = jnp.zeros((8, G), jnp.float32)
-    part_pad = jnp.concatenate([part, jnp.zeros((8, G), jnp.int32)], axis=0)
-    ret_pad = jnp.concatenate([ret, extra], axis=0)
-    rel_pad = jnp.concatenate([rel, extra], axis=0)
-    tab_c = flat(sum(near, []))
-    tab_b = flat(inner)
-    held, fresh = pl.pallas_call(
-        functools.partial(inner_kernel, sizes, len(inner)),
-        out_shape=(rows_of(8 * TILES), rows_of(SLOTS + 8)),
-        in_specs=[SM] * 2 + [VM] * 4,
-        out_specs=(VM,) * 2,
-        scratch_shapes=work_scratch(sum(sizes)),
-        compiler_params=PARAMS,
-        name="inner",
-    )(tab_b, tab_c, st, part_pad, ret_pad, rel_pad)
+    )(st, part, ret, rel, za, zb, ya, yb, held)
+    xa, xb, order_x = *swap((xa, xb), "gx"), xa
+    held = contacts((0, 2), held, order_x, "contact_near")
 
     far = contact_tables(True)
-    far = [pad(rows, UNROLL[k] if k else 16, (0, 0, zero, ZERO_AT, ZERO_AT)) for k, rows in enumerate(far)]
+    far = [pad(rows, UNROLL[k], (0, 0, zero, ZERO_AT, ZERO_AT)) for k, rows in enumerate(far)]
     sizes = tuple(len(rows) for rows in far)
-    outward = pad(outward, BATCH, (0, 0, zero, zero, zero))
-    inward = pad(inward, BATCH, (0, 0, ZERO_AT, ZERO_AT, ZERO_AT))
     forces, film_next, fresh = pl.pallas_call(
         functools.partial(halo_kernel, sizes, len(outward), len(inward)),
         out_shape=(
@@ -619,15 +683,26 @@
             rows_of(TILES),
             rows_of(SLOTS + 8),
         ),
-        in_specs=[SM] * 3 + [VM] * 5 + [AN] * 7,
+        in_specs=[SM] * 4 + [VM] * 5 + [AN] * 7,
         out_specs=(VM,) * 3,
-        scratch_shapes=work_scratch(sum(sizes))
-        + [pltpu.VMEM((HALO_ROWS, G), jnp.float32), pltpu.SemaphoreType.DMA((7,))],
+        scratch_shapes=bridge_scratch()
+        + tiles_scratch(2)
+        + contact_scratch(sum(sizes), True)
+        + [
+            pltpu.VMEM((HALO_ROWS, G), jnp.float32),
+            pltpu.VMEM((8, G), jnp.int32),
+            pltpu.SMEM((len(outward) + BATCH,), jnp.int32),
+            pltpu.SMEM((len(inward) + BATCH,), jnp.int32),
+            pltpu.SMEM((8, G), jnp.int32),
+            pltpu.SemaphoreType.DMA((8,)),
+        ],
         compiler_params=PARAMS,
         name="halo",
     )(
-        flat(outward), flat(inward), flat(sum(far, [])),
-        st, part_pad, ret_pad, rel_pad, held, fresh, za, zb, ya, yb, xa, xb,
+        flat(outward + [dummy]),
+        flat(inward + [(0, 0, ZERO_AT, ZERO_AT, ZERO_AT)]),
+        flat(sum(far, [])),
+        flags, st, part_pad, ret_pad, rel_pad, held, fresh, za, zb, ya, yb, xa, xb,
     )
     return (
         forces.reshape(positions.shape),

time: 89.3 us -> 63.9 us (0.72); the launches traced: 87.7 us -> 64.8 us
  Pallas kernels: 59.3 us -> 45.4 us
  waiting for transfers between devices: 12.6 us -> 1.75 us
  starting transfers between devices: 10.2 us -> 12 us
    ppermute x6, waiting for transfers between devices: 12.6 us -> 1.75 us  [swap(): return (lax.ppermute(first, axis, near), lax.ppermute(second, axis, far))]
    pallas_call x1, Pallas kernels: 31.9 us -> 24.7 us  [shards(): pl.pallas_call(functools.partial(halo_kernel, sizes, len(outward), len(in...]
    pallas_call x1 -> x3, Pallas kernels: 26.5 us -> 19.8 us  [the longest x2 12 us: contacts(): pl.pallas_call(functools.partial(body, sizes), out_shape=rows_of(8 * TILE...]
    ppermute x6, starting transfers between devices: 10.2 us -> 12 us  [swap(): return (lax.ppermute(first, axis, near), lax.ppermute(second, axis, far))]
  transfers between devices with their start and end apart: 6 -> 6, of which waited for: 3 -> 1; matrix products, arithmetic and copies ran while one was open for 0% -> 0% of each run, Pallas kernels for 30% -> 30%
where the time goes in v2:
time: 63.9 us; the launch traced here: 64.8 us
  Pallas kernels  45.4 us (71%)
  starting transfers between devices  12 us (19%)
  local copies, waits for them, and re-layouts  2.37 us (4%)
  other arithmetic  2.27 us (4%)
  waiting for transfers between devices  1.75 us (3%)
  between operations  0.93 us (1%)
    pallas_call x1, Pallas kernels, shards(): pl.pallas_call(functools.partial(halo_kernel, sizes, len(outward), len(in...  24.7 us
    pallas_call x2, Pallas kernels, contacts(): pl.pallas_call(functools.partial(body, sizes), out_shape=rows_of(8 * TILE...  12 us
    ppermute x6, starting transfers between devices, swap(): return (lax.ppermute(first, axis, near), lax.ppermute(second, axis, far))  12 us
    pallas_call x1, Pallas kernels, shards(): pl.pallas_call(functools.partial(bridge_kernel, len(inner)), out_shape=(r...  7.73 us
    ppermute x6, waiting for transfers between devices, swap(): return (lax.ppermute(first, axis, near), lax.ppermute(second, axis, far))  1.75 us
    unnamed x22, local copies, waits for them, and re-layouts  1.48 us
    select_n x1, other arithmetic, shards(): rel = jnp.where(live & broken, vol, 0.0)  1.38 us
  transfers between devices with their start and end apart: 6, of which 1 were waited for; matrix products, arithmetic and copies ran while one was open for 0% of the time, Pallas kernels for 30%

profile of v2, /device:TPU:108, one launch (start us, length us, event | category | flops | bytes accessed | tf_op | source)
XLA Modules:
  0.0 64.8 jit_solution(9966407172629361510)
XLA Ops:
  0.6 0.7 %reduce.live = s32[864]{0:T(1024)S(1)} reduce(s32[1,1,1,864]{3,2,1,0:T(1,128)} %param.16, s32[]{:T(128)} %constant.8.clone.1), dimensions={0,1,2}, to_apply=%param.16.reduce_sub_computation | reduce | bytes 6916 | tf_op args[3]
  1.3 0.0 copy-start.10
  1.4 1.4 %bitcast_select_fusion = (f32[864,128]{1,0:T(8,128)S(1)}, pred[1,1,1,864,128]{4,3,2,1,0:T(8,128)(4,1)S(1)}) fusion(f32[1,1,1,864,128]{4,3,2,1,0:T(8,128)} %param.19, pred[864]{0:T(1024)(128)(4,1)S(1)} %broadcast_compare_fusion.1, s32[1,1,1,864,128]{4,3,2,1,0:T(8,128)} %param.18), kind=kLoop, calls=%fused_computation | loop fusion | flops 331776 | bytes 1438560 | tf_op jit(solution)/shard_map/jit(_where)/select_n | solution.py:596
  2.8 0.0 copy-start
  2.8 0.0 copy-start.1
  2.8 0.0 copy-start.2
  2.8 0.0 copy-start.3
  2.8 0.2 bitcast_select_fusion.1.ret
  3.0 0.8 %copy-done = s32[1,1,1,864,128]{4,3,2,1,0:T(8,128)S(1)} copy-done((s32[1,1,1,864,128]{4,3,2,1,0:T(8,128)S(1)}, s32[1,1,1,864,128]{4,3,2,1,0:T(8,128)}, u32[]{:S(2)}) %copy-start) | copy-done | bytes 442392
  3.8 0.1 pack_z.1
  3.9 1.3 %collective-permute-start = (f32[512,128]{1,0:T(8,128)S(1)}, f32[512,128]{1,0:T(8,128)S(1)}, u32[]{:S(2)}, u32[]{:S(2)}) collective-permute-start(f32[512,128]{1,0:T(8,128)S(1)} %get-tuple-element.16), channel_id=1, source_target_pairs={{0,1},{1,0},{2,3},{3,2},{4,5},{5,4},{6,7},{7,6},{8,9},{9,8},{10,11... | collective-permute-start | bytes 786440 | tf_op jit(solution)/shard_map/ppermute | solution.py:562
  5.2 1.9 %collective-permute-start.1 = (f32[512,128]{1,0:T(8,128)S(1)}, f32[512,128]{1,0:T(8,128)S(1)}, u32[]{:S(2)}, u32[]{:S(2)}) collective-permute-start(f32[512,128]{1,0:T(8,128)S(1)} %get-tuple-element.17), channel_id=1, source_target_pairs={{1,2},{2,1},{5,6},{6,5},{9,10},{10,9},{13,14},{14,13},{17,18},{18,... | collective-permute-start | bytes 786440 | tf_op jit(solution)/shard_map/ppermute | solution.py:562
  7.1 0.0 copy-start.9
  7.2 0.6 copy-done.9
  7.8 5.2 %contact_own.1.after.before = f32[256,128]{1,0:T(8,128)S(1)} custom-call(s32[400]{0:T(512)S(1)} %copy-done.9, f32[256,128]{1,0:T(8,128)S(1)} %get-tuple-element.15.st.after, f32[872,128]{1,0:T(8,128)S(1)} %concatenate.10.ret, f32[872,128]{1,0:T(8,128)S(1)} %concatenate.11.rel, f32[256,128]{1,0:T(8,128)S(1)} %get-tuple-element.15.st.after), custom_call_target="tpu_custom_call" | custom-call | tf_op jit(solution)/shard_map/contact_own/pallas_call | solution.py:625
  13.1 1.7 %collective-permute-done.1.zb = f32[512,128]{1,0:T(8,128)S(1)} collective-permute-done((f32[512,128]{1,0:T(8,128)S(1)}, f32[512,128]{1,0:T(8,128)S(1)}, u32[]{:S(2)}, u32[]{:S(2)}) %collective-permute-start.1) | collective-permute-done | bytes 262176 | tf_op jit(solution)/shard_map/ppermute | solution.py:562
  14.8 0.2 pack_y.1
  15.0 1.9 %collective-permute-start.3 = (f32[384,128]{1,0:T(8,128)S(1)}, f32[384,128]{1,0:T(8,128)S(1)}, u32[]{:S(2)}, u32[]{:S(2)}) collective-permute-start(f32[384,128]{1,0:T(8,128)S(1)} %get-tuple-element.20), channel_id=1, source_target_pairs={{4,8},{8,4},{12,16},{16,12},{20,24},{24,20},{28,32},{32,28},{36,40... | collective-permute-start | bytes 589832 | tf_op jit(solution)/shard_map/ppermute | solution.py:562
  16.9 0.0 copy-start.8
  16.9 3.3 %collective-permute-start.2 = (f32[384,128]{1,0:T(8,128)S(1)}, f32[384,128]{1,0:T(8,128)S(1)}, u32[]{:S(2)}, u32[]{:S(2)}) collective-permute-start(f32[384,128]{1,0:T(8,128)S(1)} %get-tuple-element.18.after), channel_id=1, source_target_pairs={{0,4},{4,0},{8,12},{12,8},{16,20},{20,16},{24,28},{28,24},{32,36},... | collective-permute-start | bytes 589832 | tf_op jit(solution)/shard_map/ppermute | solution.py:562
  20.3 7.7 %bridge_own.1 = (f32[256,128]{1,0:T(8,128)S(1)}, f32[872,128]{1,0:T(8,128)S(1)}) custom-call(s32[2005]{0:T(1024)S(1)} %copy-done.8, s32[864]{0:T(1024)S(1)} %reduce.live, f32[256,128]{1,0:T(8,128)S(1)} %get-tuple-element.15.st.after, s32[872,128]{1,0:T(8,128)S(1)} %concatenate.9.part, f32[872,128]{1,0:T(8,128)S(1)} %concatenate.10.ret, ...), custom_call_target="tpu_custom_call" | custom-call | tf_op jit(solution)/shard_map/bridge_own/pallas_call | solution.py:649
  28.0 0.0 collective-permute-done.3.yb
  28.1 0.0 copy-start.7
  28.1 0.7 %pack_x.1 = (f32[480,128]{1,0:T(8,128)S(1)}, f32[480,128]{1,0:T(8,128)S(1)}) custom-call(f32[256,128]{1,0:T(8,128)S(1)} %get-tuple-element.15.st.after, s32[864,128]{1,0:T(8,128)S(1)} %bitcast.23, f32[864,128]{1,0:T(8,128)S(1)} %bitcast_select_fusion.1.ret, f32[864,128]{1,0:T(8,128)S(1)} %get-tuple-element.27.rel, f32[512,128]{1,0:T(8,128)S(1)} %collective-permute-done.za, ...), custom_call_target="tpu_custom_call" | custom-call | tf_op jit(solution)/shard_map/pack_x/pallas_call | solution.py:660
  28.8 3.5 %collective-permute-start.5 = (f32[480,128]{1,0:T(8,128)S(1)}, f32[480,128]{1,0:T(8,128)S(1)}, u32[]{:S(2)}, u32[]{:S(2)}) collective-permute-start(f32[480,128]{1,0:T(8,128)S(1)} %get-tuple-element.23), channel_id=1, source_target_pairs={{64,128},{128,64},{65,129},{129,65},{66,130},{130,66},{67,131},{13... | collective-permute-start | bytes 737288 | tf_op jit(solution)/shard_map/ppermute | solution.py:562
  32.3 0.0 copy-start.4
  32.3 0.0 copy-start.5
  32.3 0.0 copy-start.6
  32.3 0.1 collective-permute-start.4
  32.4 6.8 %contact_near.1.held = f32[256,128]{1,0:T(8,128)S(1)} custom-call(s32[1600]{0:T(1024)S(1)} %copy-done.7, f32[256,128]{1,0:T(8,128)S(1)} %get-tuple-element.15.st.after, f32[872,128]{1,0:T(8,128)S(1)} %concatenate.10.ret, f32[872,128]{1,0:T(8,128)S(1)} %concatenate.11.rel, f32[256,128]{1,0:T(8,128)S(1)} %get-tuple-element.19.after.before, ...), custom_call_target="tpu_custom_call" | custom-call | tf_op jit(solution)/shard_map/contact_near/pallas_call | solution.py:625
  39.3 24.7 %halo.1 = (f32[3,32,128]{2,1,0:T(8,128)}, f32[32,128]{1,0:T(8,128)}, f32[872,128]{1,0:T(8,128)S(1)}) custom-call(s32[2325]{0:T(1024)S(1)} %copy-done.6, s32[2325]{0:T(1024)S(1)} %copy-done.5, s32[2320]{0:T(1024)S(1)} %copy-done.4, s32[864]{0:T(1024)S(1)} %reduce.live, f32[256,128]{1,0:T(8,128)S(1)} %get-tuple-element.15.st.after, ...), custom_call_target="tpu_custom_call" | custom-call | tf_op jit(solution)/shard_map/halo/pallas_call | solution.py:679
  64.0 0.8 %slice_bitcast_fusion = f32[1,1,1,864,128]{4,3,2,1,0:T(8,128)} fusion(f32[872,128]{1,0:T(8,128)S(1)} %get-tuple-element.26), kind=kLoop, calls=%fused_computation.2 | loop fusion | bytes 884736 | tf_op jit(solution)/shard_map/reshape | solution.py:710
  (17 shorter events, 0.1 us)
Async XLA Ops:
  1.3 1.4 %copy-start.10 = (f32[1,1,1,864,128]{4,3,2,1,0:T(8,128)S(1)}, f32[1,1,1,864,128]{4,3,2,1,0:T(8,128)}, u32[]{:S(2)}) copy-start(f32[1,1,1,864,128]{4,3,2,1,0:T(8,128)} %param.19) | copy-start | bytes 1327108
  2.8 1.0 %copy-start = (s32[1,1,1,864,128]{4,3,2,1,0:T(8,128)S(1)}, s32[1,1,1,864,128]{4,3,2,1,0:T(8,128)}, u32[]{:S(2)}) copy-start(s32[1,1,1,864,128]{4,3,2,1,0:T(8,128)} %param.17) | copy-start | bytes 1327108
  2.8 1.0 %copy-start.1 = (f32[3,4,4,2,128]{4,3,2,1,0:T(2,128)S(1)}, f32[3,4,4,2,128]{4,3,2,1,0:T(2,128)}, u32[]{:S(2)}) copy-start(f32[3,4,4,2,128]{4,3,2,1,0:T(2,128)} %param.13) | copy-start | bytes 147460
  2.8 1.0 %copy-start.2 = (f32[4,4,2,128]{3,2,1,0:T(2,128)S(1)}, f32[4,4,2,128]{3,2,1,0:T(2,128)}, u32[]{:S(2)}) copy-start(f32[4,4,2,128]{3,2,1,0:T(2,128)} %param.14) | copy-start | bytes 49156
  2.8 1.0 %copy-start.3 = (f32[4,4,2,128]{3,2,1,0:T(2,128)S(1)}, f32[4,4,2,128]{3,2,1,0:T(2,128)}, u32[]{:S(2)}) copy-start(f32[4,4,2,128]{3,2,1,0:T(2,128)} %param.15) | copy-start | bytes 49156
  3.9 9.2 %collective-permute-start = (f32[512,128]{1,0:T(8,128)S(1)}, f32[512,128]{1,0:T(8,128)S(1)}, u32[]{:S(2)}, u32[]{:S(2)}) collective-permute-start(f32[512,128]{1,0:T(8,128)S(1)} %get-tuple-element.16), channel_id=1, source_target_pairs={{0,1},{1,0},{2,3},{3,2},{4,5},{5,4},{6,7},{7,6},{8,9},{9,8},{10,11... | collective-permute-start | bytes 786440 | tf_op jit(solution)/shard_map/ppermute | solution.py:562
  5.2 9.6 %collective-permute-start.1 = (f32[512,128]{1,0:T(8,128)S(1)}, f32[512,128]{1,0:T(8,128)S(1)}, u32[]{:S(2)}, u32[]{:S(2)}) collective-permute-start(f32[512,128]{1,0:T(8,128)S(1)} %get-tuple-element.17), channel_id=1, source_target_pairs={{1,2},{2,1},{5,6},{6,5},{9,10},{10,9},{13,14},{14,13},{17,18},{18,... | collective-permute-start | bytes 786440 | tf_op jit(solution)/shard_map/ppermute | solution.py:562
  7.1 0.7 %copy-start.9 = (s32[400]{0:T(512)S(1)}, s32[400]{0:T(512)}, u32[]{:S(2)}) copy-start(s32[400]{0:T(512)} %constant.10.clone.tab) | copy-start | bytes 4804
  15.0 13.0 %collective-permute-start.3 = (f32[384,128]{1,0:T(8,128)S(1)}, f32[384,128]{1,0:T(8,128)S(1)}, u32[]{:S(2)}, u32[]{:S(2)}) collective-permute-start(f32[384,128]{1,0:T(8,128)S(1)} %get-tuple-element.20), channel_id=1, source_target_pairs={{4,8},{8,4},{12,16},{16,12},{20,24},{24,20},{28,32},{32,28},{36,40... | collective-permute-start | bytes 589832 | tf_op jit(solution)/shard_map/ppermute | solution.py:562
  16.9 3.4 %copy-start.8 = (s32[2005]{0:T(1024)S(1)}, s32[2005]{0:T(1024)}, u32[]{:S(2)}) copy-start(s32[2005]{0:T(1024)} %constant.6.clone.tab_b) | copy-start | bytes 24064
  16.9 11.1 %collective-permute-start.2 = (f32[384,128]{1,0:T(8,128)S(1)}, f32[384,128]{1,0:T(8,128)S(1)}, u32[]{:S(2)}, u32[]{:S(2)}) collective-permute-start(f32[384,128]{1,0:T(8,128)S(1)} %get-tuple-element.18.after), channel_id=1, source_target_pairs={{0,4},{4,0},{8,12},{12,8},{16,20},{20,16},{24,28},{28,24},{32,36},... | collective-permute-start | bytes 589832 | tf_op jit(solution)/shard_map/ppermute | solution.py:562
  28.1 4.4 %copy-start.7 = (s32[1600]{0:T(1024)S(1)}, s32[1600]{0:T(1024)}, u32[]{:S(2)}) copy-start(s32[1600]{0:T(1024)} %constant.7.clone.tab_c) | copy-start | bytes 19204
  28.8 10.4 %collective-permute-start.5 = (f32[480,128]{1,0:T(8,128)S(1)}, f32[480,128]{1,0:T(8,128)S(1)}, u32[]{:S(2)}, u32[]{:S(2)}) collective-permute-start(f32[480,128]{1,0:T(8,128)S(1)} %get-tuple-element.23), channel_id=1, source_target_pairs={{64,128},{128,64},{65,129},{129,65},{66,130},{130,66},{67,131},{13... | collective-permute-start | bytes 737288 | tf_op jit(solution)/shard_map/ppermute | solution.py:562
  32.3 7.0 %copy-start.4 = (s32[2320]{0:T(1024)S(1)}, s32[2320]{0:T(1024)}, u32[]{:S(2)}) copy-start(s32[2320]{0:T(1024)} %constant.24.clone.tab_c) | copy-start | bytes 27844
  32.3 7.0 %copy-start.5 = (s32[2325]{0:T(1024)S(1)}, s32[2325]{0:T(1024)}, u32[]{:S(2)}) copy-start(s32[2325]{0:T(1024)} %constant.23.clone.tab_i) | copy-start | bytes 27904
  32.3 7.0 %copy-start.6 = (s32[2325]{0:T(1024)S(1)}, s32[2325]{0:T(1024)}, u32[]{:S(2)}) copy-start(s32[2325]{0:T(1024)} %constant.22.clone.tab_o) | copy-start | bytes 27904
  32.3 6.9 %collective-permute-start.4 = (f32[480,128]{1,0:T(8,128)S(1)}, f32[480,128]{1,0:T(8,128)S(1)}, u32[]{:S(2)}, u32[]{:S(2)}) collective-permute-start(f32[480,128]{1,0:T(8,128)S(1)} %get-tuple-element.21.after), channel_id=1, source_target_pairs={{0,64},{64,0},{128,192},{192,128},{1,65},{65,1},{129,193},{193,129... | collective-permute-start | bytes 737288 | tf_op jit(solution)/shard_map/ppermute | solution.py:562

commit v3 on v2

--- a/solution.py
+++ b/solution.py
@@ -21,7 +21,7 @@
 X_AT = Y_AT + 2 * Y_ROWS
 ZERO_AT = X_AT + 2 * X_ROWS
 HALO_ROWS = ZERO_AT + 8
-BATCH = 32
+BATCH = 64
 OFFSETS = [(i, j, k) for i in (-1, 0, 1) for j in (-1, 0, 1) for k in (-1, 0, 1)]
 
 
@@ -137,18 +137,23 @@
     return ref[pl.ds(pl.multiple_of(at, 8), 8), :]
 
 
-def compact(count, listed, jobs):
-    def body(i, n):
-        for u in range(16):
-            j = i * 16 + u
-            jobs[n] = j
-            n = n + listed(j)
+class Listing:
+    def __init__(self, count, listed, jobs):
+        self.count, self.listed, self.jobs = count, listed, jobs
+
+    def share(self, i, steps, n):
+        each = -(-self.count // steps)
+        assert each * steps == self.count
+        for u in range(each):
+            j = i * each + u
+            self.jobs[n] = j
+            n = n + self.listed(j)
         return n
 
-    n = lax.fori_loop(0, count // 16, body, 0)
-    for u in range(BATCH):
-        jobs[n + u] = count
-    return (n + BATCH - 1) // BATCH
+    def close(self, n):
+        for u in range(BATCH):
+            self.jobs[n + u] = self.count
+        return (n + BATCH - 1) // BATCH
 
 
 def run_bridges(batches, jobs, tab, a_ref, b_ref, p_ref, q_ref, l_ref, scr, acc_a, acc_b, next_ref):
@@ -208,18 +213,23 @@
                 next_ref[pl.ds(p, 1), :] = g_ref[8 * j + 4 : 8 * j + 5, :]
         if acc_b is not None:
             sub = lax.broadcasted_iota(jnp.int32, (G, G), 0)
-            for j in range(BATCH):
-                a, b, p, q, l = at[j]
-                idx = row(p_ref, p).astype(jnp.int32)
-                choose = (sub == idx).astype(jnp.bfloat16)
+            none = jnp.zeros((8, G), jnp.float32)
+            for j in range(0, BATCH, 2):
+                left, choose = [], []
+                for h in range(2):
+                    idx = row(p_ref, at[j + h][2]).astype(jnp.int32)
+                    choose.append((sub == idx).astype(jnp.bfloat16))
+                    value = f_ref[8 * (j + h) : 8 * (j + h) + 8, :]
+                    left.append(jnp.concatenate([none] * h + [value] + [none] * (1 - h), axis=1))
                 landed = lax.dot_general(
-                    f_ref[8 * j : 8 * j + 8, :].astype(jnp.bfloat16),
-                    choose,
+                    jnp.concatenate(left, axis=0).astype(jnp.bfloat16),
+                    jnp.concatenate(choose, axis=1),
                     (((1,), (1,)), ((), ())),
                     preferred_element_type=jnp.float32,
                 )
-                here = pl.ds(pl.multiple_of(b, 8), 8)
-                acc_b[here, :] = acc_b[here, :] + landed
+                for h in range(2):
+                    here = pl.ds(pl.multiple_of(at[j + h][1], 8), 8)
+                    acc_b[here, :] = acc_b[here, :] + landed[8 * h : 8 * h + 8, :]
         return carry
 
     lax.fori_loop(0, batches, body, 0)
@@ -243,7 +253,9 @@
     return [push * delta[c] for c in range(3)]
 
 
-def run_contacts(sizes, tab, t_ref, n_ref, q_ref, l_ref, nq_ref, nl_ref, low, high, mark, keys, seen, acc):
+def run_contacts(sizes, tab, t_ref, n_ref, q_ref, l_ref, nq_ref, nl_ref, low, high, mark, keys, seen, acc, beside=()):
+    beside = dict(beside)
+    lists = {}
     total = sum(sizes)
     step = max(k for k in range(1, 81) if total % k == 0)
     wide = lax.broadcasted_iota(jnp.int32, (8, G), 0)
@@ -265,9 +277,15 @@
             mark[pl.ds(j, 1), :] = jnp.where(
                 live & (distance <= limit * limit), 1.0, 0.0
             )
+        if "near" in beside:
+            carry = beside["near"].share(i, total // step, carry)
         return carry
 
-    lax.fori_loop(0, total // step, near, 0)
+    n = lax.fori_loop(0, total // step, near, 0)
+    if "near" in beside:
+        lists["near"] = beside["near"].close(n)
+    if "marked" in beside:
+        beside["marked"]()
     lane = lax.broadcasted_iota(jnp.int32, (G, G), 1)
     sub = lax.broadcasted_iota(jnp.int32, (G, G), 0)
     upper = (sub <= lane).astype(jnp.bfloat16)
@@ -313,9 +331,15 @@
         def body(i, carry, start=start, kind=kind, unroll=unroll):
             for u in range(unroll):
                 job(start + i * unroll + u, [8.0 * c for c in range(CHUNKS[kind])])
+            if kind in beside:
+                carry = beside[kind].share(i, size // unroll, carry)
             return carry
 
-        lax.fori_loop(0, size // unroll, body, 0)
+        if kind in beside and "ready" in beside:
+            beside["ready"]()
+        n = lax.fori_loop(0, size // unroll, body, 0)
+        if kind in beside:
+            lists[kind] = beside[kind].close(n)
         start += size
 
     for kind, start, size, over in crowded:
@@ -330,6 +354,8 @@
                 return lax.fori_loop(CHUNKS[kind], 16, one, carry)
 
             lax.fori_loop(0, size, rest, 0)
+
+    return lists
 
 
 def bounds(st_ref, low, high):
@@ -352,39 +378,44 @@
     return rows
 
 
-def contact_kernel(sizes, tab_c, st, ret, rel, before, after, total, *scr):
-    low, high, mark, keys, acc = scr
+def first_kernel(sizes, tab_c, st, ret, rel, after, low, high, acc, mark, keys):
     acc[...] = jnp.zeros_like(acc)
     bounds(st, low, high)
     run_contacts(sizes, tab_c, st, st, ret, rel, ret, rel, low, high, mark, keys, None, acc)
-    rows = settle(acc)
+
+
+def bridge_kernel(
+    sizes, count, tab_c, tab_b, live, st, part, ret, rel, low, high, before, after,
+    acc, acc_a, fresh, *scr
+):
+    *bridge, acc_b, mark, keys, jobs = scr
+    acc[...] = before[...]
+    acc_a[...] = jnp.zeros_like(acc_a)
+    acc_b[...] = jnp.zeros_like(acc_b)
+    fresh[...] = jnp.zeros_like(fresh)
+    listing = Listing(count, lambda j: live[tab_b[j * 5 + 2]], jobs)
+    lists = run_contacts(
+        sizes, tab_c, st, st, ret, rel, ret, rel, low, high, mark, keys, None, acc,
+        beside={3: listing},
+    )
+    run_bridges(lists[3], jobs, tab_b, st, st, part, ret, rel, bridge, acc_a, acc_b, fresh)
     for t in range(TILES):
         at = 8 * t
-        total[at : at + 8, :] = jnp.zeros((8, G), jnp.float32) if before is None else before[at : at + 8, :]
-        for c in range(3):
-            total[at + c : at + c + 1, :] = total[at + c : at + c + 1, :] + rows[3 * t + c]
-
-
-def bridge_kernel(count, tab_b, live, st, part, ret, rel, before, after, total, fresh, *scr):
-    *bridge, acc_a, acc_b, jobs = scr
-    acc_a[...] = before[...]
-    acc_b[...] = jnp.zeros_like(acc_b)
-    fresh[...] = jnp.zeros_like(fresh)
-    batches = compact(count, lambda j: live[tab_b[j * 5 + 2]], jobs)
-    run_bridges(batches, jobs, tab_b, st, st, part, ret, rel, bridge, acc_a, acc_b, fresh)
-    for t in range(TILES):
-        at = 8 * t
-        total[at : at + 4, :] = (
+        acc_a[at : at + 4, :] = (
             acc_a[at : at + 4, :] + acc_b[at : at + 4, :] + acc_b[at + 4 : at + 8, :]
         )
-        total[at + 4 : at + 8, :] = jnp.zeros((4, G), jnp.float32)
+
+
+def third_kernel(sizes, tab_c, st, ret, rel, low, high, before, after, acc, mark, keys):
+    acc[...] = before[...]
+    run_contacts(sizes, tab_c, st, st, ret, rel, ret, rel, low, high, mark, keys, None, acc)
 
 
 def halo_kernel(
-    sizes, n_out, n_in, tab_o, tab_i, tab_c, live, st, part, ret, rel, held, before,
-    za, zb, ya, yb, xa, xb, forces, film, fresh, *scr
+    sizes, n_out, n_in, tab_o, tab_i, tab_c, live, st, part, ret, rel, low, high, held, pushed,
+    before, za, zb, ya, yb, xa, xb, forces, film, fresh, *scr
 ):
-    *bridge, acc_a, acc_b, low, high, mark, keys, seen, acc, halo, flag, jobs_o, jobs_i, flags, sems = scr
+    (*bridge, acc_a, acc_b, mark, keys, seen, acc, halo, store, flag, jobs_o, jobs_i, flags, sems) = scr
     copies = []
     for k, (pair, axis, at, rows) in enumerate(
         (((za, zb), "gz", Z_AT, Z_ROWS), ((ya, yb), "gy", Y_AT, Y_ROWS), ((xa, xb), "gx", X_AT, X_ROWS))
@@ -397,35 +428,45 @@
             )
             copy.start()
             copies.append(copy)
-    keep = pltpu.make_async_copy(before, fresh, sems.at[6])
+    keep = pltpu.make_async_copy(before, store, sems.at[6])
     keep.start()
     acc_a[...] = held[...]
     acc_b[...] = jnp.zeros_like(acc_b)
-    acc[...] = jnp.zeros_like(acc)
+    acc[...] = pushed[...]
     halo[ZERO_AT : ZERO_AT + 8, :] = jnp.zeros((8, G), jnp.float32)
-    bounds(st, low, high)
-    out_batches = compact(n_out, lambda j: live[tab_o[j * 5 + 2]], jobs_o)
+    seen[sum(sizes) :, :] = jnp.zeros((512 - sum(sizes), G), jnp.float32)
     for copy in copies:
         copy.wait()
+    down = pltpu.make_async_copy(flag, flags, sems.at[7])
+
+    def marked():
+        first = (
+            lax.broadcasted_iota(jnp.int32, (8, G), 0) + lax.broadcasted_iota(jnp.int32, (8, G), 1)
+        ) == 0
+        listed = lax.dot_general(
+            first.astype(jnp.bfloat16),
+            (seen[...] > 0.0).astype(jnp.bfloat16),
+            (((1,), (1,)), ((), ())),
+            preferred_element_type=jnp.float32,
+        )
+        for k in range(4):
+            flag[k : k + 1, :] = listed[0:1, k * G : k * G + G].astype(jnp.int32)
+        down.start()
+
+    lists = run_contacts(
+        sizes, tab_c, st, halo, ret, rel, halo, halo, low, high, mark, keys, seen, acc,
+        beside={
+            "near": Listing(n_out, lambda j: live[tab_o[j * 5 + 2]], jobs_o),
+            "marked": marked,
+            "ready": down.wait,
+            0: Listing(n_in, lambda j: flags[j // G, j % G], jobs_i),
+        },
+    )
     keep.wait()
-    run_contacts(sizes, tab_c, st, halo, ret, rel, halo, halo, low, high, mark, keys, seen, acc)
-    first = (
-        lax.broadcasted_iota(jnp.int32, (8, G), 0) + lax.broadcasted_iota(jnp.int32, (8, G), 1)
-    ) == 0
-    listed = lax.dot_general(
-        first.astype(jnp.bfloat16),
-        (seen[...] > 0.0).astype(jnp.bfloat16),
-        (((1,), (1,)), ((), ())),
-        preferred_element_type=jnp.float32,
-    )
-    for k in range(4):
-        flag[k : k + 1, :] = listed[0:1, k * G : k * G + G].astype(jnp.int32)
-    down = pltpu.make_async_copy(flag, flags, sems.at[7])
-    down.start()
-    run_bridges(out_batches, jobs_o, tab_o, st, halo, part, ret, rel, bridge, acc_a, None, fresh)
-    down.wait()
-    in_batches = compact(n_in, lambda j: flags[j // G, j % G], jobs_i)
-    run_bridges(in_batches, jobs_i, tab_i, halo, st, halo, halo, halo, bridge, None, acc_b, None)
+    run_bridges(lists["near"], jobs_o, tab_o, st, halo, part, ret, rel, bridge, acc_a, None, store)
+    leave = pltpu.make_async_copy(store.at[pl.ds(0, SLOTS), :], fresh, sems.at[6])
+    leave.start()
+    run_bridges(lists[0], jobs_i, tab_i, halo, st, halo, halo, halo, bridge, None, acc_b, None)
     rows = settle(acc)
     for t in range(TILES):
         at = 8 * t
@@ -433,6 +474,7 @@
         for c in range(3):
             forces[c, t : t + 1, :] = value[c : c + 1, :] + rows[3 * t + c]
         film[t : t + 1, :] = value[3:4, :] + st[at + 4 : at + 5, :]
+    leave.wait()
 
 
 def send_sides(axis):
@@ -577,11 +619,8 @@
     return [pltpu.VMEM((8 * TILES, G), jnp.float32)] * count
 
 
-def contact_scratch(jobs, halo):
-    out = tiles_scratch(2) + [pltpu.VMEM((jobs, G), jnp.float32)] * 2
-    if halo:
-        out = out + [pltpu.VMEM((512, G), jnp.float32)]
-    return out + [pltpu.VMEM((24 * TILES, G), jnp.float32)]
+def contact_scratch(jobs):
+    return [pltpu.VMEM((jobs, G), jnp.float32)] * 2
 
 
 def shards(positions, grain_radii, film_liquid, pair_live, partner, rupture, volume):
@@ -610,32 +649,28 @@
     rel_pad = jnp.concatenate([rel, extra], axis=0)
     flags = pair_live.reshape(SLOTS)
 
-    def contacts(kinds, before, after, name):
+    def near_jobs(kinds):
         near = contact_tables(False)
         near = [
             pad(near[k], UNROLL[k], (0, 0, zero, zero, zero)) if k in kinds else [] for k in range(4)
         ]
-        sizes = tuple(len(rows) for rows in near)
-        body = contact_kernel
-        if before is None:
-            body = lambda sizes, tab, st, ret, rel, after, *rest: contact_kernel(
-                sizes, tab, st, ret, rel, None, after, *rest
-            )
-        given = [] if before is None else [before]
-        return pl.pallas_call(
-            functools.partial(body, sizes),
-            out_shape=rows_of(8 * TILES),
-            in_specs=[SM] + [VM] * (3 + len(given)) + [AN],
-            out_specs=VM,
-            scratch_shapes=contact_scratch(sum(sizes), False),
-            compiler_params=PARAMS,
-            name=name,
-        )(flat(sum(near, [])), st, ret_pad, rel_pad, *given, after)
+        return tuple(len(rows) for rows in near), flat(sum(near, []))
 
     inner, outward, inward = bridge_tables()
     dummy = (0, 0, zero, zero, zero)
+    sums = rows_of(24 * TILES)
+    tile_rows = rows_of(8 * TILES)
     za, zb = swap((za, zb), "gz")
-    held = contacts((3, 1), None, st, "contact_own")
+    sizes, tab = near_jobs((0, 1))
+    low, high, pushed = pl.pallas_call(
+        functools.partial(first_kernel, sizes),
+        out_shape=(tile_rows, tile_rows, sums),
+        in_specs=[SM] + [VM] * 3 + [AN],
+        out_specs=(VM,) * 3,
+        scratch_shapes=contact_scratch(sum(sizes)),
+        compiler_params=PARAMS,
+        name="first",
+    )(tab, st, ret_pad, rel_pad, st)
     ya, yb = pl.pallas_call(
         pack_y_kernel,
         out_shape=(rows_of(Y_ROWS),) * 2,
@@ -644,19 +679,22 @@
         scratch_shapes=[pltpu.VMEM((2 * Z_ROWS, G), jnp.float32), pltpu.SemaphoreType.DMA((2,))],
         compiler_params=PARAMS,
         name="pack_y",
-    )(st, part, ret, rel, za, zb, held)
-    ya, yb, order_y = *swap((ya, yb), "gy"), ya
-    held, fresh = pl.pallas_call(
-        functools.partial(bridge_kernel, len(inner)),
-        out_shape=(rows_of(8 * TILES), rows_of(SLOTS + 8)),
-        in_specs=[SM] * 2 + [VM] * 5 + [AN],
-        out_specs=(VM,) * 2,
+    )(st, part, ret, rel, za, zb, pushed)
+    order_y = ya
+    ya, yb = swap((ya, yb), "gy")
+    sizes, tab = near_jobs((3,))
+    pushed, held, fresh = pl.pallas_call(
+        functools.partial(bridge_kernel, sizes, len(inner)),
+        out_shape=(sums, tile_rows, rows_of(SLOTS + 8)),
+        in_specs=[SM] * 3 + [VM] * 7 + [AN],
+        out_specs=(VM,) * 3,
         scratch_shapes=bridge_scratch()
-        + tiles_scratch(2)
+        + tiles_scratch(1)
+        + contact_scratch(sum(sizes))
         + [pltpu.SMEM((len(inner) + BATCH,), jnp.int32)],
         compiler_params=PARAMS,
         name="bridge_own",
-    )(flat(inner + [dummy]), flags, st, part_pad, ret_pad, rel_pad, held, order_y)
+    )(tab, flat(inner + [dummy]), flags, st, part_pad, ret_pad, rel_pad, low, high, pushed, order_y)
     xa, xb = pl.pallas_call(
         pack_x_kernel,
         out_shape=(rows_of(X_ROWS),) * 2,
@@ -670,26 +708,40 @@
         compiler_params=PARAMS,
         name="pack_x",
     )(st, part, ret, rel, za, zb, ya, yb, held)
-    xa, xb, order_x = *swap((xa, xb), "gx"), xa
-    held = contacts((0, 2), held, order_x, "contact_near")
+    order_x = xa
+    xa, xb = swap((xa, xb), "gx")
+    sizes, tab = near_jobs((2,))
+    pushed = pl.pallas_call(
+        functools.partial(third_kernel, sizes),
+        out_shape=sums,
+        in_specs=[SM] + [VM] * 6 + [AN],
+        out_specs=VM,
+        scratch_shapes=contact_scratch(sum(sizes)),
+        compiler_params=PARAMS,
+        name="third",
+    )(tab, st, ret_pad, rel_pad, low, high, pushed, order_x)
 
     far = contact_tables(True)
     far = [pad(rows, UNROLL[k], (0, 0, zero, ZERO_AT, ZERO_AT)) for k, rows in enumerate(far)]
     sizes = tuple(len(rows) for rows in far)
+    inward = pad(inward, 5, (0, 0, ZERO_AT, ZERO_AT, ZERO_AT))
     forces, film_next, fresh = pl.pallas_call(
         functools.partial(halo_kernel, sizes, len(outward), len(inward)),
         out_shape=(
             jax.ShapeDtypeStruct((3, TILES, G), jnp.float32),
             rows_of(TILES),
-            rows_of(SLOTS + 8),
+            rows_of(SLOTS),
         ),
-        in_specs=[SM] * 4 + [VM] * 5 + [AN] * 7,
-        out_specs=(VM,) * 3,
+        in_specs=[SM] * 4 + [VM] * 8 + [AN] * 7,
+        out_specs=(VM, VM, AN),
         scratch_shapes=bridge_scratch()
         + tiles_scratch(2)
-        + contact_scratch(sum(sizes), True)
+        + contact_scratch(sum(sizes))
         + [
+            pltpu.VMEM((512, G), jnp.float32),
+            pltpu.VMEM((24 * TILES, G), jnp.float32),
             pltpu.VMEM((HALO_ROWS, G), jnp.float32),
+            pltpu.VMEM((SLOTS + 8, G), jnp.float32),
             pltpu.VMEM((8, G), jnp.int32),
             pltpu.SMEM((len(outward) + BATCH,), jnp.int32),
             pltpu.SMEM((len(inward) + BATCH,), jnp.int32),
@@ -702,12 +754,13 @@
         flat(outward + [dummy]),
         flat(inward + [(0, 0, ZERO_AT, ZERO_AT, ZERO_AT)]),
         flat(sum(far, [])),
-        flags, st, part_pad, ret_pad, rel_pad, held, fresh, za, zb, ya, yb, xa, xb,
+        flags, st, part_pad, ret_pad, rel_pad, low, high, held, pushed, fresh,
+        za, zb, ya, yb, xa, xb,
     )
     return (
         forces.reshape(positions.shape),
         film_next.reshape(film_liquid.shape),
-        fresh[:SLOTS].reshape(volume.shape),
+        fresh.reshape(volume.shape),
     )
 
 

time: 63.9 us -> 59.3 us (0.928)
  the two profiles are of different devices: /device:TPU:108 before, /device:TPU:180 now
where the time goes in v3:
time: 59.3 us; the launch traced here: 58.9 us
  Pallas kernels  38.7 us (65%)
  starting transfers between devices  8.3 us (14%)
  waiting for transfers between devices  6.43 us (11%)
  other arithmetic  2.27 us (4%)
  local copies, waits for them, and re-layouts  2.27 us (4%)
  between operations  0.9 us (2%)
    pallas_call x1, Pallas kernels, shards(): pl.pallas_call(functools.partial(halo_kernel, sizes, len(outward), len(in...  21 us
    pallas_call x1, Pallas kernels, shards(): pl.pallas_call(functools.partial(bridge_kernel, sizes, len(inner)), out_s...  8.41 us
    ppermute x6, starting transfers between devices, swap(): return (lax.ppermute(first, axis, near), lax.ppermute(second, axis, far))  8.3 us
    ppermute x6, waiting for transfers between devices, swap(): return (lax.ppermute(first, axis, near), lax.ppermute(second, axis, far))  6.43 us
    pallas_call x1, Pallas kernels, shards(): pl.pallas_call(functools.partial(first_kernel, sizes), out_shape=(tile_ro...  5.25 us
    pallas_call x1, Pallas kernels, shards(): pl.pallas_call(functools.partial(third_kernel, sizes), out_shape=sums, in...  3.12 us
    unnamed x24, local copies, waits for them, and re-layouts  2.17 us
    select_n x1, other arithmetic, shards(): rel = jnp.where(live & broken, vol, 0.0)  1.38 us
  transfers between devices with their start and end apart: 6, of which 3 were waited for; matrix products, arithmetic and copies ran while one was open for 0% of the time, Pallas kernels for 28%

profile of v3, /device:TPU:180, one launch (start us, length us, event | category | flops | bytes accessed | tf_op | source)
XLA Modules:
  0.0 58.9 jit_solution(15127756249675139889)
XLA Ops:
  0.6 0.7 %reduce.live = s32[864]{0:T(1024)S(1)} reduce(s32[1,1,1,864]{3,2,1,0:T(1,128)} %param.17, s32[]{:T(128)} %constant.9.clone.1), dimensions={0,1,2}, to_apply=%param.17.reduce_sub_computation | reduce | bytes 6916 | tf_op args[3]
  1.3 0.0 copy-start.11
  1.4 1.4 %bitcast_select_fusion = (f32[864,128]{1,0:T(8,128)S(1)}, pred[1,1,1,864,128]{4,3,2,1,0:T(8,128)(4,1)S(1)}) fusion(f32[1,1,1,864,128]{4,3,2,1,0:T(8,128)} %param.20, pred[864]{0:T(1024)(128)(4,1)S(1)} %broadcast_compare_fusion.1, s32[1,1,1,864,128]{4,3,2,1,0:T(8,128)} %param.19), kind=kLoop, calls=%fused_computation | loop fusion | flops 331776 | bytes 1438560 | tf_op jit(solution)/shard_map/jit(_where)/select_n | solution.py:635
  2.8 0.0 copy-start.2
  2.8 0.2 bitcast_select_fusion.1.ret
  3.0 0.8 %copy-done = s32[1,1,1,864,128]{4,3,2,1,0:T(8,128)S(1)} copy-done((s32[1,1,1,864,128]{4,3,2,1,0:T(8,128)S(1)}, s32[1,1,1,864,128]{4,3,2,1,0:T(8,128)}, u32[]{:S(2)}) %copy-start) | copy-done | bytes 442392
  3.8 0.1 pack_z.1
  3.9 1.3 %collective-permute-start = (f32[512,128]{1,0:T(8,128)S(1)}, f32[512,128]{1,0:T(8,128)S(1)}, u32[]{:S(2)}, u32[]{:S(2)}) collective-permute-start(f32[512,128]{1,0:T(8,128)S(1)} %get-tuple-element.23), channel_id=1, source_target_pairs={{0,1},{1,0},{2,3},{3,2},{4,5},{5,4},{6,7},{7,6},{8,9},{9,8},{10,11... | collective-permute-start | bytes 786440 | tf_op jit(solution)/shard_map/ppermute | solution.py:604
  5.2 1.9 %collective-permute-start.1 = (f32[512,128]{1,0:T(8,128)S(1)}, f32[512,128]{1,0:T(8,128)S(1)}, u32[]{:S(2)}, u32[]{:S(2)}) collective-permute-start(f32[512,128]{1,0:T(8,128)S(1)} %get-tuple-element.24), channel_id=1, source_target_pairs={{1,2},{2,1},{5,6},{6,5},{9,10},{10,9},{13,14},{14,13},{17,18},{18,... | collective-permute-start | bytes 786440 | tf_op jit(solution)/shard_map/ppermute | solution.py:604
  7.1 0.0 copy-start.8
  7.2 0.6 %copy-done.8 = s32[1440]{0:T(1024)S(1)} copy-done((s32[1440]{0:T(1024)S(1)}, s32[1440]{0:T(1024)}, u32[]{:S(2)}) %copy-start.8) | copy-done | bytes 5784
  7.8 5.2 %first.1 = (f32[256,128]{1,0:T(8,128)S(1)}, f32[256,128]{1,0:T(8,128)S(1)}, f32[768,128]{1,0:T(8,128)S(1)}) custom-call(s32[1440]{0:T(1024)S(1)} %copy-done.8, f32[256,128]{1,0:T(8,128)S(1)} %get-tuple-element.19.st.after, f32[872,128]{1,0:T(8,128)S(1)} %concatenate.10.ret, f32[872,128]{1,0:T(8,128)S(1)} %concatenate.11.rel, ...), custom_call_target="tpu_custom_call" | custom-call | tf_op jit(solution)/shard_map/first/pallas_call | solution.py:665
  13.1 1.7 %collective-permute-done.1.zb = f32[512,128]{1,0:T(8,128)S(1)} collective-permute-done((f32[512,128]{1,0:T(8,128)S(1)}, f32[512,128]{1,0:T(8,128)S(1)}, u32[]{:S(2)}, u32[]{:S(2)}) %collective-permute-start.1) | collective-permute-done | bytes 262176 | tf_op jit(solution)/shard_map/ppermute | solution.py:604
  14.8 0.2 pack_y.1
  15.0 0.1 collective-permute-start.2
  15.1 3.0 %collective-permute-start.3 = (f32[384,128]{1,0:T(8,128)S(1)}, f32[384,128]{1,0:T(8,128)S(1)}, u32[]{:S(2)}, u32[]{:S(2)}) collective-permute-start(f32[384,128]{1,0:T(8,128)S(1)} %get-tuple-element.28), channel_id=1, source_target_pairs={{4,8},{8,4},{12,16},{16,12},{20,24},{24,20},{28,32},{32,28},{36,40... | collective-permute-start | bytes 589832 | tf_op jit(solution)/shard_map/ppermute | solution.py:604
  18.1 0.0 copy-start.7
  18.2 0.0 copy-start.10
  18.2 0.6 %copy-done.7 = s32[2005]{0:T(1024)S(1)} copy-done((s32[2005]{0:T(1024)S(1)}, s32[2005]{0:T(1024)}, u32[]{:S(2)}) %copy-start.7) | copy-done | bytes 8044
  18.8 0.0 copy-done.10
  18.8 8.4 %bridge_own.1 = (f32[768,128]{1,0:T(8,128)S(1)}, f32[256,128]{1,0:T(8,128)S(1)}, f32[872,128]{1,0:T(8,128)S(1)}) custom-call(s32[160]{0:T(256)S(1)} %copy-done.10, s32[2005]{0:T(1024)S(1)} %copy-done.7, s32[864]{0:T(1024)S(1)} %reduce.live, f32[256,128]{1,0:T(8,128)S(1)} %get-tuple-element.19.st.after, s32[872,128]{1,0:T(8,128)S(1)} %concatenate.9.part, ...), custom_call_target="tpu_custom_call" | custom-call | tf_op jit(solution)/shard_map/bridge_own/pallas_call | solution.py:686
  27.3 0.7 %pack_x.1 = (f32[480,128]{1,0:T(8,128)S(1)}, f32[480,128]{1,0:T(8,128)S(1)}) custom-call(f32[256,128]{1,0:T(8,128)S(1)} %get-tuple-element.19.st.after, s32[864,128]{1,0:T(8,128)S(1)} %bitcast.22, f32[864,128]{1,0:T(8,128)S(1)} %bitcast_select_fusion.1.ret, f32[864,128]{1,0:T(8,128)S(1)} %get-tuple-element.35.rel, f32[512,128]{1,0:T(8,128)S(1)} %collective-permute-done.za, ...), custom_call_target="tpu_custom_call" | custom-call | tf_op jit(solution)/shard_map/pack_x/pallas_call | solution.py:698
  28.0 0.0 copy-start.9
  28.0 0.1 collective-permute-start.4
  28.1 1.9 %collective-permute-start.5 = (f32[480,128]{1,0:T(8,128)S(1)}, f32[480,128]{1,0:T(8,128)S(1)}, u32[]{:S(2)}, u32[]{:S(2)}) collective-permute-start(f32[480,128]{1,0:T(8,128)S(1)} %get-tuple-element.31), channel_id=1, source_target_pairs={{64,128},{128,64},{65,129},{129,65},{66,130},{130,66},{67,131},{13... | collective-permute-start | bytes 737288 | tf_op jit(solution)/shard_map/ppermute | solution.py:604
  30.0 0.0 copy-start.4
  30.0 0.0 copy-start.5
  30.1 0.0 copy-start.6
  30.1 3.1 %third.1.pushed = f32[768,128]{1,0:T(8,128)S(1)} custom-call(s32[400]{0:T(512)S(1)} %copy-done.9, f32[256,128]{1,0:T(8,128)S(1)} %get-tuple-element.19.st.after, f32[872,128]{1,0:T(8,128)S(1)} %concatenate.10.ret, f32[872,128]{1,0:T(8,128)S(1)} %concatenate.11.rel, f32[256,128]{1,0:T(8,128)S(1)} %get-tuple-element.20.low, ...), custom_call_target="tpu_custom_call" | custom-call | tf_op jit(solution)/shard_map/third/pallas_call | solution.py:714
  33.2 1.8 %collective-permute-done.4.xa = f32[480,128]{1,0:T(8,128)S(1)} collective-permute-done((f32[480,128]{1,0:T(8,128)S(1)}, f32[480,128]{1,0:T(8,128)S(1)}, u32[]{:S(2)}, u32[]{:S(2)}) %collective-permute-start.4) | collective-permute-done | bytes 245792 | tf_op jit(solution)/shard_map/ppermute | solution.py:604
  35.0 2.9 %collective-permute-done.5.xb = f32[480,128]{1,0:T(8,128)S(1)} collective-permute-done((f32[480,128]{1,0:T(8,128)S(1)}, f32[480,128]{1,0:T(8,128)S(1)}, u32[]{:S(2)}, u32[]{:S(2)}) %collective-permute-start.5) | collective-permute-done | bytes 245792 | tf_op jit(solution)/shard_map/ppermute | solution.py:604
  37.9 21.0 %halo.1 = (f32[3,32,128]{2,1,0:T(8,128)}, f32[32,128]{1,0:T(8,128)}, f32[864,128]{1,0:T(8,128)}) custom-call(s32[2325]{0:T(1024)S(1)} %copy-done.4, s32[2330]{0:T(1024)S(1)} %copy-done.5, s32[2320]{0:T(1024)S(1)} %copy-done.6, s32[864]{0:T(1024)S(1)} %reduce.live, f32[256,128]{1,0:T(8,128)S(1)} %get-tuple-element.19.st.after, ...), custom_call_target="tpu_custom_call" | custom-call | tf_op jit(solution)/shard_map/halo/pallas_call | solution.py:728
  (18 shorter events, 0.1 us)
Async XLA Ops:
  1.3 1.4 %copy-start.11 = (f32[1,1,1,864,128]{4,3,2,1,0:T(8,128)S(1)}, f32[1,1,1,864,128]{4,3,2,1,0:T(8,128)}, u32[]{:S(2)}) copy-start(f32[1,1,1,864,128]{4,3,2,1,0:T(8,128)} %param.20) | copy-start | bytes 1327108
  2.8 1.0 %copy-start = (s32[1,1,1,864,128]{4,3,2,1,0:T(8,128)S(1)}, s32[1,1,1,864,128]{4,3,2,1,0:T(8,128)}, u32[]{:S(2)}) copy-start(s32[1,1,1,864,128]{4,3,2,1,0:T(8,128)} %param.18) | copy-start | bytes 1327108
  2.8 1.0 %copy-start.1 = (f32[3,4,4,2,128]{4,3,2,1,0:T(2,128)S(1)}, f32[3,4,4,2,128]{4,3,2,1,0:T(2,128)}, u32[]{:S(2)}) copy-start(f32[3,4,4,2,128]{4,3,2,1,0:T(2,128)} %param.14) | copy-start | bytes 147460
  2.8 1.0 %copy-start.2 = (f32[4,4,2,128]{3,2,1,0:T(2,128)S(1)}, f32[4,4,2,128]{3,2,1,0:T(2,128)}, u32[]{:S(2)}) copy-start(f32[4,4,2,128]{3,2,1,0:T(2,128)} %param.15) | copy-start | bytes 49156
  2.8 1.0 %copy-start.3 = (f32[4,4,2,128]{3,2,1,0:T(2,128)S(1)}, f32[4,4,2,128]{3,2,1,0:T(2,128)}, u32[]{:S(2)}) copy-start(f32[4,4,2,128]{3,2,1,0:T(2,128)} %param.16) | copy-start | bytes 49156
  3.9 9.2 %collective-permute-start = (f32[512,128]{1,0:T(8,128)S(1)}, f32[512,128]{1,0:T(8,128)S(1)}, u32[]{:S(2)}, u32[]{:S(2)}) collective-permute-start(f32[512,128]{1,0:T(8,128)S(1)} %get-tuple-element.23), channel_id=1, source_target_pairs={{0,1},{1,0},{2,3},{3,2},{4,5},{5,4},{6,7},{7,6},{8,9},{9,8},{10,11... | collective-permute-start | bytes 786440 | tf_op jit(solution)/shard_map/ppermute | solution.py:604
  5.2 9.6 %collective-permute-start.1 = (f32[512,128]{1,0:T(8,128)S(1)}, f32[512,128]{1,0:T(8,128)S(1)}, u32[]{:S(2)}, u32[]{:S(2)}) collective-permute-start(f32[512,128]{1,0:T(8,128)S(1)} %get-tuple-element.24), channel_id=1, source_target_pairs={{1,2},{2,1},{5,6},{6,5},{9,10},{10,9},{13,14},{14,13},{17,18},{18,... | collective-permute-start | bytes 786440 | tf_op jit(solution)/shard_map/ppermute | solution.py:604
  7.1 0.7 %copy-start.8 = (s32[1440]{0:T(1024)S(1)}, s32[1440]{0:T(1024)}, u32[]{:S(2)}) copy-start(s32[1440]{0:T(1024)} %constant.11.clone.tab_c) | copy-start | bytes 17284
  15.0 12.3 %collective-permute-start.2 = (f32[384,128]{1,0:T(8,128)S(1)}, f32[384,128]{1,0:T(8,128)S(1)}, u32[]{:S(2)}, u32[]{:S(2)}) collective-permute-start(f32[384,128]{1,0:T(8,128)S(1)} %get-tuple-element.25.after), channel_id=1, source_target_pairs={{0,4},{4,0},{8,12},{12,8},{16,20},{20,16},{24,28},{28,24},{32,36},... | collective-permute-start | bytes 589832 | tf_op jit(solution)/shard_map/ppermute | solution.py:604
  15.1 12.2 %collective-permute-start.3 = (f32[384,128]{1,0:T(8,128)S(1)}, f32[384,128]{1,0:T(8,128)S(1)}, u32[]{:S(2)}, u32[]{:S(2)}) collective-permute-start(f32[384,128]{1,0:T(8,128)S(1)} %get-tuple-element.28), channel_id=1, source_target_pairs={{4,8},{8,4},{12,16},{16,12},{20,24},{24,20},{28,32},{32,28},{36,40... | collective-permute-start | bytes 589832 | tf_op jit(solution)/shard_map/ppermute | solution.py:604
  18.1 0.7 %copy-start.7 = (s32[2005]{0:T(1024)S(1)}, s32[2005]{0:T(1024)}, u32[]{:S(2)}) copy-start(s32[2005]{0:T(1024)} %constant.8.clone.tab_b) | copy-start | bytes 24064
  18.2 0.7 %copy-start.10 = (s32[160]{0:T(256)S(1)}, s32[160]{0:T(256)}, u32[]{:S(2)}) copy-start(s32[160]{0:T(256)} %constant.7.clone.tab_c) | copy-start | bytes 1924
  28.0 2.0 %copy-start.9 = (s32[400]{0:T(512)S(1)}, s32[400]{0:T(512)}, u32[]{:S(2)}) copy-start(s32[400]{0:T(512)} %constant.24.clone.tab_c) | copy-start | bytes 4804
  28.0 7.0 %collective-permute-start.4 = (f32[480,128]{1,0:T(8,128)S(1)}, f32[480,128]{1,0:T(8,128)S(1)}, u32[]{:S(2)}, u32[]{:S(2)}) collective-permute-start(f32[480,128]{1,0:T(8,128)S(1)} %get-tuple-element.29.after), channel_id=1, source_target_pairs={{0,64},{64,0},{128,192},{192,128},{1,65},{65,1},{129,193},{193,129... | collective-permute-start | bytes 737288 | tf_op jit(solution)/shard_map/ppermute | solution.py:604
  28.1 9.8 %collective-permute-start.5 = (f32[480,128]{1,0:T(8,128)S(1)}, f32[480,128]{1,0:T(8,128)S(1)}, u32[]{:S(2)}, u32[]{:S(2)}) collective-permute-start(f32[480,128]{1,0:T(8,128)S(1)} %get-tuple-element.31), channel_id=1, source_target_pairs={{64,128},{128,64},{65,129},{129,65},{66,130},{130,66},{67,131},{13... | collective-permute-start | bytes 737288 | tf_op jit(solution)/shard_map/ppermute | solution.py:604
  30.0 7.9 %copy-start.4 = (s32[2325]{0:T(1024)S(1)}, s32[2325]{0:T(1024)}, u32[]{:S(2)}) copy-start(s32[2325]{0:T(1024)} %constant.25.clone.tab_o) | copy-start | bytes 27904
  30.0 7.9 %copy-start.5 = (s32[2330]{0:T(1024)S(1)}, s32[2330]{0:T(1024)}, u32[]{:S(2)}) copy-start(s32[2330]{0:T(1024)} %constant.26.clone.tab_i) | copy-start | bytes 27964
  30.1 7.8 %copy-start.6 = (s32[2320]{0:T(1024)S(1)}, s32[2320]{0:T(1024)}, u32[]{:S(2)}) copy-start(s32[2320]{0:T(1024)} %constant.27.clone.tab_c) | copy-start | bytes 27844

commit v4 on v3

--- a/solution.py
+++ b/solution.py
@@ -210,7 +210,7 @@
                 a, b, p, q, l = at[j]
                 here = pl.ds(pl.multiple_of(a, 8), 8)
                 acc_a[here, :] = acc_a[here, :] + g_ref[8 * j : 8 * j + 8, :]
-                next_ref[pl.ds(p, 1), :] = g_ref[8 * j + 4 : 8 * j + 5, :]
+                next_ref[pl.ds(q, 1), :] = g_ref[8 * j + 4 : 8 * j + 5, :]
         if acc_b is not None:
             sub = lax.broadcasted_iota(jnp.int32, (G, G), 0)
             none = jnp.zeros((8, G), jnp.float32)
@@ -486,7 +486,42 @@
     return [ref[pl.ds(at, 9), :].astype(jnp.float32) for ref in refs]
 
 
-def pack_z_kernel(pos, rad, film, part, ret, rel, st, out_a, out_b):
+def pack_z_kernel(
+    pos_in, rad_in, film_in, live_in, part_in, broken_in, vol_in, st, part, ret, rel, out_a, out_b,
+    pos, rad, film, live, broken, vol, sems,
+):
+    copies = [
+        pltpu.make_async_copy(src, dst, sems.at[k])
+        for k, (src, dst) in enumerate(
+            (
+                (live_in, live), (broken_in, broken), (vol_in, vol), (part_in, part),
+                (pos_in, pos), (rad_in, rad), (film_in, film),
+            )
+        )
+    ]
+    for copy in copies:
+        copy.start()
+    for copy in copies:
+        copy.wait()
+    flags = [live[0:1, G * k : G * k + G] for k in range(SLOTS // G)]
+    rest = SLOTS - G * (SLOTS // G)
+    flags.append(
+        jnp.concatenate(
+            [live[0:1, SLOTS - rest : SLOTS], jnp.zeros((1, G - rest), jnp.int32)], axis=1
+        )
+    )
+    flags.append(jnp.zeros((8 - len(flags), G), jnp.int32))
+    columns = jnp.transpose(jnp.concatenate(flags, axis=0).astype(jnp.float32))
+    for k in range(SLOTS // G + 1):
+        count = min(G, SLOTS - G * k)
+        here = slice(G * k, G * k + count)
+        listed = jnp.broadcast_to(columns[0:count, k : k + 1], (count, G)) > 0.0
+        lost = broken[here, :] > 0
+        held = jnp.where(listed, vol[here, :], 0.0)
+        ret[here, :] = jnp.where(lost, 0.0, held)
+        rel[here, :] = jnp.where(lost, held, 0.0)
+    for ref in (ret, rel):
+        ref[SLOTS : SLOTS + 8, :] = jnp.zeros((8, G), jnp.float32)
     for g in range(TILES // 8):
         members = [pos[c, 8 * g : 8 * g + 8, :] for c in range(3)]
         members += [rad[8 * g : 8 * g + 8, :], film[8 * g : 8 * g + 8, :]]
@@ -629,24 +664,38 @@
     film = film_liquid.reshape(TILES, G)
     part = partner.reshape(SLOTS, G)
     vol = volume.reshape(SLOTS, G)
-    live = pair_live.reshape(SLOTS, 1) > 0
-    broken = rupture.reshape(SLOTS, G) > 0
-    ret = jnp.where(live & ~broken, vol, 0.0)
-    rel = jnp.where(live & broken, vol, 0.0)
-
-    st, za, zb = pl.pallas_call(
+    broken = rupture.reshape(SLOTS, G)
+
+    st, part, ret, rel, za, zb = pl.pallas_call(
         pack_z_kernel,
-        out_shape=(rows_of(8 * TILES), rows_of(Z_ROWS), rows_of(Z_ROWS)),
-        in_specs=[VM] * 6,
-        out_specs=(VM,) * 3,
+        out_shape=(
+            rows_of(8 * TILES),
+            jax.ShapeDtypeStruct((SLOTS, G), jnp.int32),
+            rows_of(SLOTS + 8),
+            rows_of(SLOTS + 8),
+            rows_of(Z_ROWS),
+            rows_of(Z_ROWS),
+        ),
+        in_specs=[pl.BlockSpec(memory_space=pltpu.HBM)] * 7,
+        out_specs=(VM,) * 6,
+        scratch_shapes=[
+            pltpu.VMEM((3, TILES, G), jnp.float32),
+            pltpu.VMEM((TILES, G), jnp.float32),
+            pltpu.VMEM((TILES, G), jnp.float32),
+            pltpu.VMEM((1, SLOTS), jnp.int32),
+            pltpu.VMEM((SLOTS, G), jnp.int32),
+            pltpu.VMEM((SLOTS, G), jnp.float32),
+            pltpu.SemaphoreType.DMA((7,)),
+        ],
         compiler_params=PARAMS,
         name="pack_z",
-    )(pos, rad, film, part, ret, rel)
+    )(
+        *[
+            pltpu.with_memory_space_constraint(value, pltpu.HBM)
+            for value in (pos, rad, film, pair_live.reshape(1, SLOTS), part, broken, vol)
+        ]
+    )
     zero = SLOTS
-    extra = jnp.zeros((8, G), jnp.float32)
-    part_pad = jnp.concatenate([part, jnp.zeros((8, G), jnp.int32)], axis=0)
-    ret_pad = jnp.concatenate([ret, extra], axis=0)
-    rel_pad = jnp.concatenate([rel, extra], axis=0)
     flags = pair_live.reshape(SLOTS)
 
     def near_jobs(kinds):
@@ -657,7 +706,7 @@
         return tuple(len(rows) for rows in near), flat(sum(near, []))
 
     inner, outward, inward = bridge_tables()
-    dummy = (0, 0, zero, zero, zero)
+    dummy = (0, 0, 0, zero, zero)
     sums = rows_of(24 * TILES)
     tile_rows = rows_of(8 * TILES)
     za, zb = swap((za, zb), "gz")
@@ -670,7 +719,7 @@
         scratch_shapes=contact_scratch(sum(sizes)),
         compiler_params=PARAMS,
         name="first",
-    )(tab, st, ret_pad, rel_pad, st)
+    )(tab, st, ret, rel, st)
     ya, yb = pl.pallas_call(
         pack_y_kernel,
         out_shape=(rows_of(Y_ROWS),) * 2,
@@ -694,7 +743,7 @@
         + [pltpu.SMEM((len(inner) + BATCH,), jnp.int32)],
         compiler_params=PARAMS,
         name="bridge_own",
-    )(tab, flat(inner + [dummy]), flags, st, part_pad, ret_pad, rel_pad, low, high, pushed, order_y)
+    )(tab, flat(inner + [dummy]), flags, st, part, ret, rel, low, high, pushed, order_y)
     xa, xb = pl.pallas_call(
         pack_x_kernel,
         out_shape=(rows_of(X_ROWS),) * 2,
@@ -719,7 +768,7 @@
         scratch_shapes=contact_scratch(sum(sizes)),
         compiler_params=PARAMS,
         name="third",
-    )(tab, st, ret_pad, rel_pad, low, high, pushed, order_x)
+    )(tab, st, ret, rel, low, high, pushed, order_x)
 
     far = contact_tables(True)
     far = [pad(rows, UNROLL[k], (0, 0, zero, ZERO_AT, ZERO_AT)) for k, rows in enumerate(far)]
@@ -754,7 +803,7 @@
         flat(outward + [dummy]),
         flat(inward + [(0, 0, ZERO_AT, ZERO_AT, ZERO_AT)]),
         flat(sum(far, [])),
-        flags, st, part_pad, ret_pad, rel_pad, low, high, held, pushed, fresh,
+        flags, st, part, ret, rel, low, high, held, pushed, fresh,
         za, zb, ya, yb, xa, xb,
     )
     return (

time: 59.3 us -> 59.4 us (level)
  the two profiles are of different devices: /device:TPU:180 before, /device:TPU:108 now
where the time goes in v4:
time: 59.4 us; the launch traced here: 59.3 us
  Pallas kernels  39.8 us (67%)
  starting transfers between devices  12 us (20%)
  waiting for transfers between devices  5.94 us (10%)
  between operations  0.82 us (1%)
  local copies, waits for them, and re-layouts  0.71 us (1%)
    pallas_call x1, Pallas kernels, shards(): pl.pallas_call(functools.partial(halo_kernel, sizes, len(outward), len(in...  20.4 us
    ppermute x6, starting transfers between devices, swap(): return (lax.ppermute(first, axis, near), lax.ppermute(second, axis, far))  12 us
    pallas_call x1, Pallas kernels, shards(): pl.pallas_call(functools.partial(bridge_kernel, sizes, len(inner)), out_s...  8.41 us
    ppermute x6, waiting for transfers between devices, swap(): return (lax.ppermute(first, axis, near), lax.ppermute(second, axis, far))  5.94 us
    pallas_call x1, Pallas kernels, shards(): pl.pallas_call(functools.partial(first_kernel, sizes), out_shape=(tile_ro...  5.25 us
    pallas_call x1, Pallas kernels, shards(): pl.pallas_call(functools.partial(third_kernel, sizes), out_shape=sums, in...  3.12 us
    pallas_call x1, Pallas kernels, shards(): pl.pallas_call(pack_z_kernel, out_shape=(rows_of(8 * TILES), jax.ShapeDty...  1.76 us
  transfers between devices with their start and end apart: 6, of which 3 were waited for; matrix products, arithmetic and copies ran while one was open for 0% of the time, Pallas kernels for 28%

profile of v4, /device:TPU:108, one launch (start us, length us, event | category | flops | bytes accessed | tf_op | source)
XLA Modules:
  0.0 59.3 jit_solution(18420636192683427695)
XLA Ops:
  0.6 1.8 %pack_z.1 = (f32[256,128]{1,0:T(8,128)S(1)}, s32[864,128]{1,0:T(8,128)S(1)}, f32[872,128]{1,0:T(8,128)S(1)}, f32[872,128]{1,0:T(8,128)S(1)}, f32[512,128]{1,0:T(8,128)S(1)}, /*index=5*/f32[512,128]{1,0:T(8,128)S(1)}) custom-call(f32[3,32,128]{2,1,0:T(8,128)} %bitcast.13, f32[32,128]{1,0:T(8,128)} %bitcast.14, f32[32,128]{1,0:T(8,128)} %bitcast.15, ...), custom_call_target="tpu_custom_call" | custom-call | tf_op jit(solution)/shard_map/pack_z/pallas_call | solution.py:669
  2.4 0.0 copy-start.4
  2.4 1.3 %collective-permute-start = (f32[512,128]{1,0:T(8,128)S(1)}, f32[512,128]{1,0:T(8,128)S(1)}, u32[]{:S(2)}, u32[]{:S(2)}) collective-permute-start(f32[512,128]{1,0:T(8,128)S(1)} %get-tuple-element.29), channel_id=1, source_target_pairs={{0,1},{1,0},{2,3},{3,2},{4,5},{5,4},{6,7},{7,6},{8,9},{9,8},{10,11... | collective-permute-start | bytes 786440 | tf_op jit(solution)/shard_map/ppermute | solution.py:639
  3.7 1.9 %collective-permute-start.1 = (f32[512,128]{1,0:T(8,128)S(1)}, f32[512,128]{1,0:T(8,128)S(1)}, u32[]{:S(2)}, u32[]{:S(2)}) collective-permute-start(f32[512,128]{1,0:T(8,128)S(1)} %get-tuple-element.30), channel_id=1, source_target_pairs={{1,2},{2,1},{5,6},{6,5},{9,10},{10,9},{13,14},{14,13},{17,18},{18,... | collective-permute-start | bytes 786440 | tf_op jit(solution)/shard_map/ppermute | solution.py:639
  5.6 0.0 copy-done.4
  5.6 5.3 %first.1 = (f32[256,128]{1,0:T(8,128)S(1)}, f32[256,128]{1,0:T(8,128)S(1)}, f32[768,128]{1,0:T(8,128)S(1)}) custom-call(s32[1440]{0:T(1024)S(1)} %copy-done.4, f32[256,128]{1,0:T(8,128)S(1)} %get-tuple-element.22.st.after, f32[872,128]{1,0:T(8,128)S(1)} %get-tuple-element.24.ret, f32[872,128]{1,0:T(8,128)S(1)} %get-tuple-element.25.rel, ...), custom_call_target="tpu_custom_call" | custom-call | tf_op jit(solution)/shard_map/first/pallas_call | solution.py:714
  10.9 0.0 collective-permute-done.za
  10.9 2.4 %collective-permute-done.1.zb = f32[512,128]{1,0:T(8,128)S(1)} collective-permute-done((f32[512,128]{1,0:T(8,128)S(1)}, f32[512,128]{1,0:T(8,128)S(1)}, u32[]{:S(2)}, u32[]{:S(2)}) %collective-permute-start.1) | collective-permute-done | bytes 262176 | tf_op jit(solution)/shard_map/ppermute | solution.py:639
  13.3 0.2 pack_y.1
  13.5 0.0 copy-start.3
  13.5 1.9 %collective-permute-start.3 = (f32[384,128]{1,0:T(8,128)S(1)}, f32[384,128]{1,0:T(8,128)S(1)}, u32[]{:S(2)}, u32[]{:S(2)}) collective-permute-start(f32[384,128]{1,0:T(8,128)S(1)} %get-tuple-element.34), channel_id=1, source_target_pairs={{4,8},{8,4},{12,16},{16,12},{20,24},{24,20},{28,32},{32,28},{36,40... | collective-permute-start | bytes 589832 | tf_op jit(solution)/shard_map/ppermute | solution.py:639
  15.5 3.3 %collective-permute-start.2 = (f32[384,128]{1,0:T(8,128)S(1)}, f32[384,128]{1,0:T(8,128)S(1)}, u32[]{:S(2)}, u32[]{:S(2)}) collective-permute-start(f32[384,128]{1,0:T(8,128)S(1)} %get-tuple-element.31.after), channel_id=1, source_target_pairs={{0,4},{4,0},{8,12},{12,8},{16,20},{20,16},{24,28},{28,24},{32,36},... | collective-permute-start | bytes 589832 | tf_op jit(solution)/shard_map/ppermute | solution.py:639
  18.8 0.0 copy-done.7
  18.8 0.0 copy-start.6
  18.8 0.0 copy-done.3
  18.8 0.7 %copy-done.6 = s32[160]{0:T(256)S(1)} copy-done((s32[160]{0:T(256)S(1)}, s32[160]{0:T(256)}, u32[]{:S(2)}) %copy-start.6) | copy-done | bytes 664
  19.5 8.4 %bridge_own.1 = (f32[768,128]{1,0:T(8,128)S(1)}, f32[256,128]{1,0:T(8,128)S(1)}, f32[872,128]{1,0:T(8,128)S(1)}) custom-call(s32[160]{0:T(256)S(1)} %copy-done.6, s32[2005]{0:T(1024)S(1)} %copy-done.3, s32[864]{0:T(1024)S(1)} %reduce.live, f32[256,128]{1,0:T(8,128)S(1)} %get-tuple-element.22.st.after, s32[864,128]{1,0:T(8,128)S(1)} %get-tuple-element.23.part, ...), custom_call_target="tpu_custom_call" | custom-call | tf_op jit(solution)/shard_map/bridge_own/pallas_call | solution.py:735
  27.9 0.0 collective-permute-done.3.yb
  27.9 0.0 collective-permute-done.2.ya
  27.9 0.7 %pack_x.1 = (f32[480,128]{1,0:T(8,128)S(1)}, f32[480,128]{1,0:T(8,128)S(1)}) custom-call(f32[256,128]{1,0:T(8,128)S(1)} %get-tuple-element.22.st.after, s32[864,128]{1,0:T(8,128)S(1)} %get-tuple-element.23.part, f32[872,128]{1,0:T(8,128)S(1)} %get-tuple-element.24.ret, f32[872,128]{1,0:T(8,128)S(1)} %get-tuple-element.25.rel, ...), custom_call_target="tpu_custom_call" | custom-call | tf_op jit(solution)/shard_map/pack_x/pallas_call | solution.py:747
  28.6 0.0 copy-start.5
  28.6 3.5 %collective-permute-start.5 = (f32[480,128]{1,0:T(8,128)S(1)}, f32[480,128]{1,0:T(8,128)S(1)}, u32[]{:S(2)}, u32[]{:S(2)}) collective-permute-start(f32[480,128]{1,0:T(8,128)S(1)} %get-tuple-element.37), channel_id=1, source_target_pairs={{64,128},{128,64},{65,129},{129,65},{66,130},{130,66},{67,131},{13... | collective-permute-start | bytes 737288 | tf_op jit(solution)/shard_map/ppermute | solution.py:639
  32.1 0.1 collective-permute-start.4
  32.2 0.0 copy-done.5
  32.2 0.0 copy-start
  32.2 0.0 copy-start.1
  32.3 0.0 copy-start.2
  32.3 3.1 %third.1.pushed = f32[768,128]{1,0:T(8,128)S(1)} custom-call(s32[400]{0:T(512)S(1)} %copy-done.5, f32[256,128]{1,0:T(8,128)S(1)} %get-tuple-element.22.st.after, f32[872,128]{1,0:T(8,128)S(1)} %get-tuple-element.24.ret, f32[872,128]{1,0:T(8,128)S(1)} %get-tuple-element.25.rel, f32[256,128]{1,0:T(8,128)S(1)} %get-tuple-element.26.low, ...), custom_call_target="tpu_custom_call" | custom-call | tf_op jit(solution)/shard_map/third/pallas_call | solution.py:763
  35.4 1.9 %collective-permute-done.5.xb = f32[480,128]{1,0:T(8,128)S(1)} collective-permute-done((f32[480,128]{1,0:T(8,128)S(1)}, f32[480,128]{1,0:T(8,128)S(1)}, u32[]{:S(2)}, u32[]{:S(2)}) %collective-permute-start.5) | collective-permute-done | bytes 245792 | tf_op jit(solution)/shard_map/ppermute | solution.py:639
  37.3 1.6 %collective-permute-done.4.xa = f32[480,128]{1,0:T(8,128)S(1)} collective-permute-done((f32[480,128]{1,0:T(8,128)S(1)}, f32[480,128]{1,0:T(8,128)S(1)}, u32[]{:S(2)}, u32[]{:S(2)}) %collective-permute-start.4) | collective-permute-done | bytes 245792 | tf_op jit(solution)/shard_map/ppermute | solution.py:639
  38.9 0.0 copy-done.1
  38.9 20.4 %halo.1 = (f32[3,32,128]{2,1,0:T(8,128)}, f32[32,128]{1,0:T(8,128)}, f32[864,128]{1,0:T(8,128)}) custom-call(s32[2325]{0:T(1024)S(1)} %copy-done.2, s32[2330]{0:T(1024)S(1)} %copy-done.1, s32[2320]{0:T(1024)S(1)} %copy-done, s32[864]{0:T(1024)S(1)} %reduce.live, f32[256,128]{1,0:T(8,128)S(1)} %get-tuple-element.22.st.after, ...), custom_call_target="tpu_custom_call" | custom-call | tf_op jit(solution)/shard_map/halo/pallas_call | solution.py:777
  (4 shorter events, 0.0 us)
Async XLA Ops:
  2.4 3.2 %copy-start.4 = (s32[1440]{0:T(1024)S(1)}, s32[1440]{0:T(1024)}, u32[]{:S(2)}) copy-start(s32[1440]{0:T(1024)} %constant.14.clone.tab_c) | copy-start | bytes 17284
  2.4 8.5 %collective-permute-start = (f32[512,128]{1,0:T(8,128)S(1)}, f32[512,128]{1,0:T(8,128)S(1)}, u32[]{:S(2)}, u32[]{:S(2)}) collective-permute-start(f32[512,128]{1,0:T(8,128)S(1)} %get-tuple-element.29), channel_id=1, source_target_pairs={{0,1},{1,0},{2,3},{3,2},{4,5},{5,4},{6,7},{7,6},{8,9},{9,8},{10,11... | collective-permute-start | bytes 786440 | tf_op jit(solution)/shard_map/ppermute | solution.py:639
  3.7 9.6 %collective-permute-start.1 = (f32[512,128]{1,0:T(8,128)S(1)}, f32[512,128]{1,0:T(8,128)S(1)}, u32[]{:S(2)}, u32[]{:S(2)}) collective-permute-start(f32[512,128]{1,0:T(8,128)S(1)} %get-tuple-element.30), channel_id=1, source_target_pairs={{1,2},{2,1},{5,6},{6,5},{9,10},{10,9},{13,14},{14,13},{17,18},{18,... | collective-permute-start | bytes 786440 | tf_op jit(solution)/shard_map/ppermute | solution.py:639
  13.3 5.4 %copy-start.7 = (s32[1,1,1,864]{3,2,1,0:T(1,128)S(1)}, s32[1,1,1,864]{3,2,1,0:T(1,128)}, u32[]{:S(2)}) copy-start(s32[1,1,1,864]{3,2,1,0:T(1,128)} %param.17) | copy-start | bytes 10372
  13.5 5.3 %copy-start.3 = (s32[2005]{0:T(1024)S(1)}, s32[2005]{0:T(1024)}, u32[]{:S(2)}) copy-start(s32[2005]{0:T(1024)} %constant.16.clone.tab_b) | copy-start | bytes 24064
  13.5 14.4 %collective-permute-start.3 = (f32[384,128]{1,0:T(8,128)S(1)}, f32[384,128]{1,0:T(8,128)S(1)}, u32[]{:S(2)}, u32[]{:S(2)}) collective-permute-start(f32[384,128]{1,0:T(8,128)S(1)} %get-tuple-element.34), channel_id=1, source_target_pairs={{4,8},{8,4},{12,16},{16,12},{20,24},{24,20},{28,32},{32,28},{36,40... | collective-permute-start | bytes 589832 | tf_op jit(solution)/shard_map/ppermute | solution.py:639
  15.5 12.4 %collective-permute-start.2 = (f32[384,128]{1,0:T(8,128)S(1)}, f32[384,128]{1,0:T(8,128)S(1)}, u32[]{:S(2)}, u32[]{:S(2)}) collective-permute-start(f32[384,128]{1,0:T(8,128)S(1)} %get-tuple-element.31.after), channel_id=1, source_target_pairs={{0,4},{4,0},{8,12},{12,8},{16,20},{20,16},{24,28},{28,24},{32,36},... | collective-permute-start | bytes 589832 | tf_op jit(solution)/shard_map/ppermute | solution.py:639
  18.8 0.7 %copy-start.6 = (s32[160]{0:T(256)S(1)}, s32[160]{0:T(256)}, u32[]{:S(2)}) copy-start(s32[160]{0:T(256)} %constant.15.clone.tab_c) | copy-start | bytes 1924
  28.6 3.6 %copy-start.5 = (s32[400]{0:T(512)S(1)}, s32[400]{0:T(512)}, u32[]{:S(2)}) copy-start(s32[400]{0:T(512)} %constant.17.clone.tab_c) | copy-start | bytes 4804
  28.6 8.7 %collective-permute-start.5 = (f32[480,128]{1,0:T(8,128)S(1)}, f32[480,128]{1,0:T(8,128)S(1)}, u32[]{:S(2)}, u32[]{:S(2)}) collective-permute-start(f32[480,128]{1,0:T(8,128)S(1)} %get-tuple-element.37), channel_id=1, source_target_pairs={{64,128},{128,64},{65,129},{129,65},{66,130},{130,66},{67,131},{13... | collective-permute-start | bytes 737288 | tf_op jit(solution)/shard_map/ppermute | solution.py:639
  32.1 6.8 %collective-permute-start.4 = (f32[480,128]{1,0:T(8,128)S(1)}, f32[480,128]{1,0:T(8,128)S(1)}, u32[]{:S(2)}, u32[]{:S(2)}) collective-permute-start(f32[480,128]{1,0:T(8,128)S(1)} %get-tuple-element.35.after), channel_id=1, source_target_pairs={{0,64},{64,0},{128,192},{192,128},{1,65},{65,1},{129,193},{193,129... | collective-permute-start | bytes 737288 | tf_op jit(solution)/shard_map/ppermute | solution.py:639
  32.2 6.7 %copy-start = (s32[2320]{0:T(1024)S(1)}, s32[2320]{0:T(1024)}, u32[]{:S(2)}) copy-start(s32[2320]{0:T(1024)} %constant.20.clone.tab_c) | copy-start | bytes 27844
  32.2 6.6 %copy-start.1 = (s32[2330]{0:T(1024)S(1)}, s32[2330]{0:T(1024)}, u32[]{:S(2)}) copy-start(s32[2330]{0:T(1024)} %constant.19.clone.tab_i) | copy-start | bytes 27964
  32.3 6.6 %copy-start.2 = (s32[2325]{0:T(1024)S(1)}, s32[2325]{0:T(1024)}, u32[]{:S(2)}) copy-start(s32[2325]{0:T(1024)} %constant.18.clone.tab_o) | copy-start | bytes 27904
